TPU v7x, 32 devices: a whole 2x2x4 slice. The times are simulated.
32 devices in a mesh: kown: 8 (over z, y), qown: 4 (over x, core).
Axes of the slice: x: 2, y: 2, z: 4, core: 2. Of those that a mesh axis runs over, the one named last changes fastest.
Arguments:
- g_coarse: bfloat16 [512, 512, 2, 1280], P('kown', 'qown'), may hold values from -384 to 384
- k_points: int32 [3, 512], replicated, may hold values from 0 to 7, as said below
- q_points: int32 [3, 512], replicated, may hold values from 0 to 7, as said below
- re_cells: int32 [3, 512], replicated, may hold values from -4 to 4, as said below
- rp_cells: int32 [3, 512], replicated, may hold values from -4 to 4, as said below
- rp_degen: int32 [512], replicated, may hold values from 1 to 4
- fine_q: int32 [3, 64], replicated, may hold values from 0 to 31
Outputs:
- fine_g: bfloat16 [512, 64, 2, 1280], P('kown', 'qown')
Inputs may be any that keep to these rules, and one draw needn't show every extreme that they name: `k_points`: the columns are the 8**3 points of the coarse grid, each once. `q_points`: the columns are the 8**3 points of the coarse grid, each once. `re_cells`: the columns reduced modulo 8 are the 8**3 points of the grid, each once. `rp_cells`: the columns reduced modulo 8 are the 8**3 points of the grid, each once.
All inputs are finite; a program needn't handle non-finite values.
Results may differ from a plain program's by a relative error of at most 0.0095.
Values may be sent and summed in bfloat16 or wider, within the bound.
No kernel may reach another device: no remote copies, remote signals or barrier semaphores. Data moves between devices by JAX's collectives and lax.ppermute only.
A program may use at most 320 MiB of HBM per device.

v0:
```python
import jax
import jax.numpy as jnp
import numpy as np
from jax import lax
from jax.sharding import PartitionSpec as P

GRID = 8
FGRID = 32


def circle(modulus):
    angles = 2.0 * np.pi * np.arange(modulus) / modulus
    return (
        jnp.asarray(np.cos(angles).astype(np.float32)),
        jnp.asarray(np.sin(angles).astype(np.float32)),
    )


def lookup(turn_index, lookup_table):
    levels = jnp.arange(lookup_table.shape[0], dtype=jnp.int32)
    return jnp.sum(
        jnp.where(turn_index[..., None] == levels, lookup_table, jnp.zeros_like(lookup_table)),
        axis=-1,
    )


def phases(left_ints, right_ints, modulus, factor):
    turn_count = jnp.mod(jnp.sum(left_ints[:, :, None] * right_ints[:, None, :], axis=0), modulus)
    cosine, sine_vals = circle(modulus)
    return (
        (lookup(turn_count, cosine) * factor).astype(jnp.bfloat16),
        (lookup(turn_count, sine_vals) * factor).astype(jnp.bfloat16),
    )


def combine(former, latter):
    real_part = former[:, :, 0] + latter[:, :, 1]
    imag_part = former[:, :, 1] - latter[:, :, 0]
    return jnp.stack([real_part, imag_part], axis=2)


def transform_rows(cosine, sine_vals, operand):
    flattened = operand.reshape(operand.shape[0], -1)
    shape_out = (cosine.shape[0],) + operand.shape[1:]
    former = jnp.dot(cosine, flattened, preferred_element_type=jnp.float32).reshape(shape_out)
    latter = jnp.dot(sine_vals, flattened, preferred_element_type=jnp.float32).reshape(shape_out)
    return combine(former, latter).astype(jnp.bfloat16)


def per_device(g_coarse, k_points, q_points, re_cells, rp_cells, rp_degen, fine_q):
    k_cosine, k_sine = phases(re_cells, k_points, GRID, 1.0 / k_points.shape[1])
    q_cosine, q_sine = phases(rp_cells, q_points, GRID, 1.0 / q_points.shape[1])
    weights = 1.0 / rp_degen.astype(jnp.float32)
    f_cosine, f_sine = phases(fine_q, rp_cells, FGRID, weights[None, :])
    f_sine = -f_sine
    k_done = transform_rows(
        k_cosine, k_sine, lax.all_to_all(g_coarse, "kown", split_axis=1, concat_axis=0, tiled=True)
    )
    arranged = lax.all_to_all(k_done, "kown", split_axis=0, concat_axis=1, tiled=True)
    operand = lax.all_to_all(arranged, "qown", split_axis=0, concat_axis=1, tiled=True)
    former = jnp.einsum("rq,eqcp->ercp", q_cosine, operand, preferred_element_type=jnp.float32)
    latter = jnp.einsum("rq,eqcp->ercp", q_sine, operand, preferred_element_type=jnp.float32)
    g_ep = combine(former, latter).astype(jnp.bfloat16)
    former = jnp.einsum("fr,ercp->efcp", f_cosine, g_ep, preferred_element_type=jnp.float32)
    latter = jnp.einsum("fr,ercp->efcp", f_sine, g_ep, preferred_element_type=jnp.float32)
    fine_grid = combine(former, latter).astype(jnp.bfloat16)
    return lax.all_to_all(fine_grid, "qown", split_axis=1, concat_axis=0, tiled=True)


def solution(mesh):
    return jax.shard_map(
        per_device,
        mesh=mesh,
        in_specs=(P("kown", "qown", None, None), P(), P(), P(), P(), P(), P()),
        out_specs=P("kown", "qown", None, None),
        check_vma=False,
    )
```

profile of v0, /device:TPU:8, one launch (start us, length us, event | category | flops | bytes accessed | tf_op | source)
XLA Modules:
  0.0 3244.0 jit_solution(16573616520939192998)
XLA Ops:
  0.0 33.6 %copy.45 = bf16[64,128,2,1280]{3,2,0,1:T(2,128)(2,1)} copy(bf16[64,128,2,1280]{3,2,1,0:T(2,128)(2,1)} %param.13) | data formatting | bytes 83886080 | tf_op args[0]
  43.1 17.9 select_reduce_fusion.3
  61.0 880.9 %all-to-all-done = bf16[64,128,2,1280]{3,2,0,1:T(2,128)(2,1)} async-done(((bf16[64,128,2,1280]{3,2,0,1:T(2,128)(2,1)}), bf16[64,128,2,1280]{3,2,0,1:T(2,128)(2,1)}, u32[]{:S(2)}, u32[]{:S(2)}) %all-to-all-start) | async-done | bytes 41943072 | tf_op jit(solution)/shard_map/all_to_all | solution.py:57
  941.9 48.0 %copy.65 = bf16[64,8,16,2,1280]{4,3,2,0,1:T(2,128)(2,1)} copy(bf16[64,8,16,2,1280]{4,3,0,2,1:T(2,128)(2,1)} %bitcast.2) | data formatting | bytes 83886080 | tf_op jit(solution)/shard_map/all_to_all | solution.py:57
  990.0 60.8 %reshape.54 = bf16[512,40960]{1,0:T(8,128)(2,1)} reshape(bf16[8,64,16,2,1280]{4,3,2,1,0:T(2,128)(2,1)} %bitcast.67) | data formatting | bytes 83886080 | tf_op jit(solution)/shard_map/reshape | solution.py:43
  1050.7 54.6 %copy.47 = bf16[40960,512]{1,0:T(8,128)(2,1)} copy(bf16[40960,512]{0,1:T(8,128)(2,1)} %bitcast.68) | data formatting | bytes 83886080 | tf_op jit(solution)/shard_map/dot_general | solution.py:45
  1105.3 57.9 %fusion.13 = f32[512,16,2,1280]{3,0,2,1:T(8,128)} fusion(bf16[16,2,1280,512]{3,2,1,0:T(8,128)(2,1)} %bitcast.64, f32[512,512]{1,0:T(8,128)S(1)} %get-tuple-element.7), kind=kOutput, calls=%fused_computation.46 | convolution fusion | flops 21475360768 | bytes 126877696 | tf_op jit(solution)/shard_map/dot_general | solution.py:45
  1163.2 58.2 %fusion.16 = f32[512,16,2,1280]{3,0,2,1:T(8,128)} fusion(bf16[16,2,1280,512]{3,2,1,0:T(8,128)(2,1)} %bitcast.65, f32[512,512]{1,0:T(8,128)S(1)} %get-tuple-element.8), kind=kOutput, calls=%fused_computation.48 | convolution fusion | flops 21475360768 | bytes 126877696 | tf_op jit(solution)/shard_map/dot_general | solution.py:46
  1221.4 67.1 %fusion.3 = (bf16[512,16,1,1280]{3,0,2,1:T(8,128)(2,1)}, bf16[512,16,1,1280]{3,0,2,1:T(8,128)(2,1)}) fusion(f32[512,16,2,1280]{3,0,2,1:T(8,128)} %fusion.16, f32[512,16,2,1280]{3,0,2,1:T(8,128)} %fusion.13), kind=kLoop, calls=%fused_computation.9 | loop fusion | flops 41943040 | bytes 209715200 | tf_op jit(solution)/shard_map/convert.4
  1288.5 28.9 pad_maximum_fusion
  1317.4 75.1 %copy.48 = bf16[512,16,2,1280]{3,2,1,0:T(2,128)(2,1)} copy(bf16[512,16,2,1280]{3,0,2,1:T(8,128)(2,1)} %pad_maximum_fusion) | data formatting | bytes 83886080 | tf_op jit(solution)/shard_map/stack | solution.py:39
  1392.4 917.3 %all_to_all.69 = bf16[512,16,2,1280]{3,2,1,0:T(2,128)(2,1)} all-to-all(bf16[512,16,2,1280]{3,2,1,0:T(2,128)(2,1)} %copy.48), channel_id=1, replica_groups=mesh['kown'=8,'qown'=4] {'kown'}, dimensions={0} | all-to-all | bytes 83886080 | tf_op jit(solution)/shard_map/all_to_all | solution.py:59
  2309.7 28.2 copy.49
  2338.0 28.5 copy.50
  2366.5 11.8 all-to-all-start.2
  2381.7 449.3 %all-to-all-done.2 = bf16[64,128,2,1280]{3,1,2,0:T(8,128)(2,1)} async-done(((bf16[64,128,2,1280]{3,1,2,0:T(8,128)(2,1)}), bf16[64,128,2,1280]{3,1,2,0:T(8,128)(2,1)}, u32[]{:S(2)}, u32[]{:S(2)}) %all-to-all-start.2) | async-done | bytes 41943072 | tf_op jit(solution)/shard_map/all_to_all | solution.py:60
  2831.0 63.2 %copy.51 = bf16[16,4,128,2,1280]{2,1,4,3,0:T(4,128)(2,1)} copy(bf16[16,4,128,2,1280]{4,2,3,0,1:T(8,128)(2,1)} %bitcast.12) | data formatting | bytes 83886080 | tf_op jit(solution)/shard_map/all_to_all | solution.py:60
  2894.2 60.3 %all_to_all.60 = bf16[16,512,2,1280]{1,3,2,0:T(8,128)(2,1)} reshape(bf16[16,4,128,2,1280]{2,1,4,3,0:T(4,128)(2,1)} %copy.51) | data formatting | bytes 83886080 | tf_op jit(solution)/shard_map/all_to_all | solution.py:60
  2954.5 44.5 %convolution_bitcast_fusion.1 = f32[16,512,2,1280]{1,3,2,0:T(8,128)} fusion(bf16[16,512,2,1280]{1,3,2,0:T(8,128)(2,1)} %all_to_all.60, f32[512,512]{1,0:T(8,128)S(1)} %copy-done.1), kind=kOutput, calls=%fused_computation.1 | convolution fusion | flops 21475360768 | bytes 126877696 | tf_op jit(solution)/shard_map/rq,eqcp->ercp/dot_general | solution.py:61
  2999.0 44.4 %convolution_bitcast_fusion = f32[16,512,2,1280]{1,3,2,0:T(8,128)} fusion(bf16[16,512,2,1280]{1,3,2,0:T(8,128)(2,1)} %all_to_all.60, f32[512,512]{1,0:T(8,128)S(1)} %copy-done), kind=kOutput, calls=%fused_computation | convolution fusion | flops 21475360768 | bytes 126877696 | tf_op jit(solution)/shard_map/rq,eqcp->ercp/dot_general | solution.py:62
  3043.3 66.4 %fusion.1 = (bf16[16,512,1,1280]{1,3,2,0:T(8,128)(2,1)}, bf16[16,512,1,1280]{1,3,2,0:T(8,128)(2,1)}) fusion(f32[16,512,2,1280]{1,3,2,0:T(8,128)} %convolution_bitcast_fusion, f32[16,512,2,1280]{1,3,2,0:T(8,128)} %convolution_bitcast_fusion.1), kind=kLoop, calls=%fused_computation.5 | loop fusion | flops 41943040 | bytes 209715200 | tf_op jit(solution)/shard_map/convert.2
  3109.8 18.4 fusion.6
  3128.2 21.4 fusion.7
  3167.4 65.7 %all_to_all.70 = bf16[16,64,2,1280]{3,2,0,1:T(2,128)(2,1)} all-to-all(bf16[16,64,2,1280]{3,2,0,1:T(2,128)(2,1)} %copy.54), channel_id=1, replica_groups=mesh['kown'=8,'qown'=4] {'qown'}, dimensions={1} | all-to-all | bytes 10485760 | tf_op jit(solution)/shard_map/all_to_all | solution.py:67
  (44 shorter events, 41.3 us)
Async XLA Ops:
  33.6 8.0 copy-start.4
  33.6 8.0 copy-start.6
  33.6 8.3 copy-start.7
  33.6 8.3 copy-start.8
  33.7 9.4 copy-start.14
  33.7 9.4 copy-start.15
  33.7 908.3 %all-to-all-start = ((bf16[64,128,2,1280]{3,2,0,1:T(2,128)(2,1)}), bf16[64,128,2,1280]{3,2,0,1:T(2,128)(2,1)}, u32[]{:S(2)}, u32[]{:S(2)}) async-start(bf16[64,128,2,1280]{3,2,0,1:T(2,128)(2,1)} %copy.45), calls=%async_computation | async-start | bytes 83886080 | tf_op jit(solution)/shard_map/all_to_all | solution.py:57
  2366.5 11.8 copy-start.5
  2366.5 11.8 copy-start.9
  2366.5 11.9 copy-start.10
  2366.5 12.6 copy-start.12
  2366.5 12.6 copy-start.13
  2366.5 464.5 %all-to-all-start.2 = ((bf16[64,128,2,1280]{3,1,2,0:T(8,128)(2,1)}), bf16[64,128,2,1280]{3,1,2,0:T(8,128)(2,1)}, u32[]{:S(2)}, u32[]{:S(2)}) async-start(bf16[64,128,2,1280]{3,1,2,0:T(8,128)(2,1)} %bitcast.66), calls=%async_computation.2 | async-start | bytes 83886080 | tf_op jit(solution)/shard_map/all_to_all | solution.py:60
  2894.2 60.3 %copy-start.1 = (f32[512,512]{1,0:T(8,128)S(1)}, f32[512,512]{1,0:T(8,128)}, u32[]{:S(2)}) copy-start(f32[512,512]{1,0:T(8,128)} %get-tuple-element.12) | copy-start | bytes 3145732
  2954.5 44.5 %copy-start = (f32[512,512]{1,0:T(8,128)S(1)}, f32[512,512]{1,0:T(8,128)}, u32[]{:S(2)}) copy-start(f32[512,512]{1,0:T(8,128)} %get-tuple-element.11) | copy-start | bytes 3145732
  3043.3 66.4 %copy-start.3 = (f32[64,512]{1,0:T(8,128)S(1)}, f32[64,512]{1,0:T(8,128)}, u32[]{:S(2)}) copy-start(f32[64,512]{1,0:T(8,128)} %get-tuple-element.9) | copy-start | bytes 393220
  3043.3 66.4 %copy-start.11 = (f32[512]{0:T(512)S(1)}, f32[512]{0:T(512)}, u32[]{:S(2)}) copy-start(f32[512]{0:T(512)} %convert_divide_fusion) | copy-start | bytes 6148
  3109.8 18.4 copy-start.2
where the time goes:
time: 3260 us; the launch traced here: 3240 us
  waiting for transfers between devices  1330 us (41%)
  blocking collectives  983 us (30%)
  local copies, waits for them, and re-layouts  473 us (15%)
  matrix products  245 us (8%)
  other arithmetic  193 us (6%)
    all_to_all x1, blocking collectives, per_device(): lax.all_to_all(k_done, 'kown', split_axis=0, concat_axis=1, tiled=True)  917 us
    all_to_all x1, waiting for transfers between devices, per_device(): lax.all_to_all(g_coarse, 'kown', split_axis=1, concat_axis=0, tiled=True)  881 us
    all_to_all x1, waiting for transfers between devices, per_device(): lax.all_to_all(arranged, 'qown', split_axis=0, concat_axis=1, tiled=True)  449 us
    another operation x3, other arithmetic  138 us
    all_to_all x2, local copies, waits for them, and re-layouts, per_device(): lax.all_to_all(arranged, 'qown', split_axis=0, concat_axis=1, tiled=True)  124 us
    another operation x2, local copies, waits for them, and re-layouts, combine(): return jnp.stack([real_part, imag_part], axis=2)  85.3 us
    all_to_all x1, blocking collectives, per_device(): lax.all_to_all(fine_grid, 'qown', split_axis=1, concat_axis=0, tiled=True)  65.7 us
  transfers between devices with their start and end apart: 2, of which 2 were waited for; matrix products, arithmetic and copies ran while one was open for 1% of the time, Pallas kernels for 0%

commit v1 on v0

v1 whole, which is shorter than its diff:
```python
import functools

import jax
import jax.numpy as jnp
import numpy as np
from jax import lax
from jax.experimental import pallas as pl
from jax.experimental.pallas import tpu as pltpu
from jax.sharding import PartitionSpec as P

GRID = 8
FGRID = 32
LANES = 128
BF16 = jnp.bfloat16
F32 = jnp.float32


def cosines(turns, modulus):
    table = np.cos(2.0 * np.pi * np.arange(modulus) / modulus).astype(np.float32)
    turns = turns & (modulus - 1)
    turns = jnp.minimum(turns, modulus - turns)
    value = jnp.full(turns.shape, table[0], F32)
    for level in range(1, modulus // 2 + 1):
        value = jnp.where(turns == level, table[level], value)
    return value


def spread(coordinates, count, index_of):
    shape = (coordinates.shape[1], count)
    wanted = index_of(lax.broadcasted_iota(jnp.int32, shape, 1))
    chosen = (lax.broadcasted_iota(jnp.int32, shape, 0) == wanted).astype(F32).astype(BF16)
    return jnp.dot(coordinates.astype(F32).astype(BF16), chosen, preferred_element_type=F32).astype(BF16)


def products(left, right):
    turns = lax.dot_general(left, right, (((0,), (0,)), ((), ())), preferred_element_type=F32)
    return turns.astype(jnp.int32)


def odd(shape, axis):
    return lax.broadcasted_iota(jnp.int32, shape, axis) & 1


def fine_weights(kown, qown, near, fine_q, rp_cells, rp_degen, q_points):
    f_total, cells, q_total = fine_q.shape[1], rp_cells.shape[1], q_points.shape[1]
    q_count = q_total // qown if near else q_total

    def kernel(f_ref, rp_ref, degen_ref, q_ref, out_ref):
        first = lax.axis_index("qown") * q_count if near else 0
        block = f_total // qown

        def fine_index(n):
            if not near:
                return n >> 1
            owner = n // (2 * block)
            owner = ((owner & 1) * (qown // 2) + (owner >> 1)) ^ lax.axis_index("qown")
            return owner * block + ((n >> 1) & (block - 1))

        rp = rp_ref[...].astype(F32).astype(BF16)
        fine = spread(f_ref[...], 2 * f_total, fine_index)
        q_near = spread(q_ref[...], 2 * q_count, lambda n: (n >> 1) + first)
        f_turns = products(fine, rp)
        q_turns = products(rp, q_near)
        scale = 1.0 / degen_ref[...].astype(F32)
        total = jnp.zeros((2 * f_total, 2 * q_count), F32)
        for part in range(2):
            f_part = cosines(f_turns + (FGRID // 4) * (part - odd(f_turns.shape, 0)), FGRID) * scale
            q_part = cosines(q_turns + (GRID // 4) * (part - odd(q_turns.shape, 1)), GRID) * (1.0 / q_total)
            total += jnp.dot(f_part.astype(BF16), q_part.astype(BF16), preferred_element_type=F32)
        out_ref[...] = total.astype(BF16)

    return pl.pallas_call(
        kernel,
        out_shape=jax.ShapeDtypeStruct((2 * f_total, 2 * q_count), BF16),
        compiler_params=pltpu.CompilerParams(vmem_limit_bytes=24 << 20),
        name="fine_weights",
    )(fine_q, rp_cells, rp_degen.reshape(1, cells), q_points)


def k_phases(kown, near, re_cells, k_points):
    cells, points = re_cells.shape[1], k_points.shape[1]
    rows = 2 * cells // kown

    def kernel(re_ref, k_ref, out_ref, columns):
        at = pl.program_id(0)
        me_k = lax.axis_index("kown") if near else 0

        @pl.when(at == 0)
        def _():
            columns[...] = spread(k_ref[...], 2 * points, lambda n: n >> 1)

        row = spread(re_ref[...], rows, lambda n: (n >> 1) + (at ^ me_k) * (cells // kown))
        turns = products(row, columns[...])
        quarter = (GRID // 4) * (odd(turns.shape, 0) - odd(turns.shape, 1))
        out_ref[...] = (cosines(turns + quarter, GRID) * (1.0 / points)).astype(BF16)

    return pl.pallas_call(
        kernel,
        grid=(kown,),
        in_specs=[pl.BlockSpec(re_cells.shape, lambda i: (0, 0)), pl.BlockSpec(k_points.shape, lambda i: (0, 0))],
        out_specs=pl.BlockSpec((rows, 2 * points), lambda i: (i, 0)),
        out_shape=jax.ShapeDtypeStruct((2 * cells, 2 * points), BF16),
        scratch_shapes=[pltpu.VMEM((3, 2 * points), BF16)],
        compiler_params=pltpu.CompilerParams(vmem_limit_bytes=24 << 20),
        name="k_phases",
    )(re_cells, k_points)


def interpolate(weights, g, start, width, pairs, per_pair):
    k_count, q_count = g.shape[:2]
    step = 8
    half = weights.shape[0] // 2

    def kernel(w_ref, g_ref, *out_refs):
        for at in range(step):
            operand = g_ref[at].reshape(2 * q_count, width)
            product = jnp.dot(w_ref[...], operand, preferred_element_type=F32).astype(BF16)
            for core in range(2):
                block = product[core * half : (core + 1) * half]
                out_refs[core][:, :, :, at] = block.reshape(2, pairs, per_pair, 2, width)

    shape = jax.ShapeDtypeStruct((2, pairs, per_pair, k_count, 2, width), BF16)
    return pl.pallas_call(
        kernel,
        grid=(k_count // step,),
        in_specs=[
            pl.BlockSpec(weights.shape, lambda i: (0, 0)),
            pl.BlockSpec(
                (pl.Element(step), pl.Element(q_count), pl.Element(2), pl.Element(width)),
                lambda i: (i * step, 0, 0, start),
            ),
        ],
        out_specs=[pl.BlockSpec((2, pairs, per_pair, step, 2, width), lambda i: (0, 0, 0, i, 0, 0))] * 2,
        out_shape=[shape] * 2,
        compiler_params=pltpu.CompilerParams(vmem_limit_bytes=12 << 20),
        name="interpolate",
    )(weights, g)


def add(name, which, *arrays):
    pairs, per_pair, k_count, _, width = arrays[0].shape[-5:]
    step = 16

    def kernel(*refs):
        for pair in range(pairs):
            for j in range(per_pair):
                total = sum(ref[pair, j].reshape(2 * step, width).astype(F32) for ref in refs[:-1])
                refs[-1][pair, j] = total.astype(BF16).reshape(step, 2, width)

    block = (pairs, per_pair, step, 2, width)
    whole = pl.BlockSpec(block, lambda i: (0, 0, i, 0, 0))
    part = pl.BlockSpec((pl.Squeezed(),) + block, lambda i: (which, 0, 0, i, 0, 0))
    return pl.pallas_call(
        kernel,
        grid=(k_count // step,),
        in_specs=[part if array.ndim == 6 else whole for array in arrays],
        out_specs=whole,
        out_shape=jax.ShapeDtypeStruct(arrays[0].shape[-5:], BF16),
        compiler_params=pltpu.CompilerParams(vmem_limit_bytes=8 << 20),
        name=name,
    )(*arrays)


def to_cells(k_matrix, rows):
    owners, per_pair, k_count, _, width = rows.shape

    def kernel(m_ref, in_ref, *out_refs):
        operand = in_ref[:, 0].reshape(owners * 2 * k_count, width)
        for at in range(owners):
            part = m_ref[at * 2 * k_count : (at + 1) * 2 * k_count, :]
            product = jnp.dot(part, operand, preferred_element_type=F32).astype(BF16)
            out_refs[at][:, 0] = product.reshape(k_count, 2, width)

    return pl.pallas_call(
        kernel,
        grid=(per_pair,),
        in_specs=[
            pl.BlockSpec(k_matrix.shape, lambda j: (0, 0)),
            pl.BlockSpec((owners, 1, k_count, 2, width), lambda j: (0, j, 0, 0, 0)),
        ],
        out_specs=[pl.BlockSpec((k_count, 1, 2, width), lambda j: (0, j, 0, 0))] * owners,
        out_shape=[jax.ShapeDtypeStruct((k_count, per_pair, 2, width), BF16)] * owners,
        compiler_params=pltpu.CompilerParams(vmem_limit_bytes=16 << 20),
        name="to_cells",
    )(k_matrix, rows)


def place(blocks, start, total, out):
    cells, per_pair, _, width = blocks[0].shape
    count = len(blocks)
    step = 16
    given = [] if out is None else [out]

    def kernel(*refs):
        ins, out_ref = refs[:count], refs[-1]
        me = lax.axis_index("kown")
        for at in range(count):
            out_ref[:, pl.ds((me ^ at) * per_pair, per_pair)] = ins[at][...]

    return pl.pallas_call(
        kernel,
        grid=(cells // step,),
        in_specs=[pl.BlockSpec((step, per_pair, 2, width), lambda i: (i, 0, 0, 0))] * count
        + [pl.BlockSpec(memory_space=pl.ANY)] * len(given),
        out_specs=pl.BlockSpec(
            (pl.Element(step), pl.Element(count * per_pair), pl.Element(2), pl.Element(width)),
            lambda i: (i * step, 0, 0, start),
        ),
        out_shape=jax.ShapeDtypeStruct((cells, count * per_pair, 2, total), BF16),
        input_output_aliases={} if out is None else {count: 0},
        compiler_params=pltpu.CompilerParams(vmem_limit_bytes=8 << 20),
        name="place",
    )(*blocks, *given)


def swap(array, axis, size, bit):
    return lax.ppermute(array, axis, [(i, i ^ bit) for i in range(size)])


def chunks_of(pairs):
    tiles = pairs // LANES
    sizes = [1, 3, 3]
    sizes = sizes + [tiles - sum(sizes)] if tiles > sum(sizes) else [tiles]
    starts = np.concatenate([[0], np.cumsum(sizes)[:-1]])
    return [(int(a) * LANES, int(b) * LANES) for a, b in zip(starts, sizes)]


def after(array, *others):
    return lax.optimization_barrier((array, *others))[0]


def order_of(count):
    order = [("S", 0), ("S", 1), ("C", 0), ("M", 0), ("C", 1), ("X", 0), ("S", 2), ("K", 0), ("C", 2), ("X", 1)]
    for at in range(1, count):
        order += [("S", at + 2), ("C", at + 2), ("X", at + 1), ("P", at - 1), ("K", at)]
    return order + [("P", count - 1)]


def pipelined(kown, qown, g, k_points, q_points, re_cells, rp_cells, rp_degen, fine_q):
    per_pair = fine_q.shape[1] // (qown * kown)
    chunks = chunks_of(g.shape[3])
    count = len(chunks)
    kept, near, sent, far, summed, rows, cells, done = {}, {}, {}, {}, {}, {}, {}, {-1: None}
    weights = fine_weights(kown, qown, True, fine_q, rp_cells, rp_degen, q_points)
    last = weights
    k_matrix = None

    def over_q(at):
        nonlocal last
        start, width = chunks[at]
        kept[at], send = interpolate(after(weights, last), g, start, width, kown, per_pair)
        near[at] = swap(send, "qown", qown, 1)
        last = kept[at]

    def add_core(at):
        nonlocal last
        sent[at] = add("add_core", 1, kept[at], after(near[at], last))
        gates = [far[at - 1]] if at == 1 and True else []
        far[at] = swap(after(sent[at], *gates), "qown", qown, 2)
        last = sent[at]

    def add_x(at):
        nonlocal last
        summed[at] = add("add_x", 0, kept[at], near[at], after(far[at], last))
        rows[at] = lax.all_to_all(summed[at], "kown", split_axis=0, concat_axis=0, tiled=True)
        last = summed[at]

    def over_k(at):
        nonlocal last
        cells[at] = to_cells(k_matrix, after(rows[at], last))
        last = cells[at][0]

    def finish(at):
        nonlocal last
        blocks = [block if by == 0 else swap(block, "kown", kown, by) for by, block in enumerate(cells[at])]
        blocks[-1] = after(blocks[-1], last)
        done[at] = place(blocks, chunks[at][0], g.shape[3], done[at - 1])
        if at + 1 < count:
            last, done[at] = lax.optimization_barrier((last, done[at]))

    stages = {"S": over_q, "C": add_core, "X": add_x, "K": over_k, "P": finish}
    for stage, at in order_of(count):
        if stage == "M":
            k_matrix = k_phases(kown, True, after(re_cells, last), k_points)
            last = k_matrix
        elif at < count:
            stages[stage](at)
    return done[count - 1]


def gathered(kown, qown, g, k_points, q_points, re_cells, rp_cells, rp_degen, fine_q):
    q_total, k_total = q_points.shape[1], k_points.shape[1]
    weights = fine_weights(kown, qown, False, fine_q, rp_cells, rp_degen, q_points)
    k_matrix = k_phases(kown, False, re_cells, k_points)
    done = []
    for start in range(0, g.shape[3], 2 * LANES):
        some = after(g, *done)[..., start : start + 2 * LANES]
        rows = lax.all_to_all(some, "qown", split_axis=0, concat_axis=1, tiled=True)
        rows = rows.reshape(rows.shape[0], 2 * q_total, -1)
        fine = jnp.einsum("fq,kqp->kfp", weights, rows, preferred_element_type=F32).astype(BF16)
        fine = lax.all_to_all(fine, "qown", split_axis=1, concat_axis=0, tiled=True)
        fine = lax.all_to_all(fine, "kown", split_axis=1, concat_axis=0, tiled=True)
        fine = fine.reshape(k_total, -1, 2, rows.shape[2]).swapaxes(0, 1).reshape(-1, 2 * k_total, rows.shape[2])
        cells = jnp.einsum("rk,fkp->frp", k_matrix, fine, preferred_element_type=F32).astype(BF16)
        done.append(lax.all_to_all(cells, "kown", split_axis=1, concat_axis=0, tiled=True))
    cells = jnp.concatenate(done, axis=2)
    return cells.reshape(cells.shape[0], -1, 2, g.shape[3]).swapaxes(0, 1)


def solution(mesh):
    kown, qown = mesh.shape["kown"], mesh.shape["qown"]

    def per_device(g_coarse, *rest):
        few = rest[-1].shape[1] <= g_coarse.shape[1]
        form = pipelined if few and qown == 4 else gathered
        return form(kown, qown, g_coarse, *rest)

    return jax.shard_map(
        per_device,
        mesh=mesh,
        in_specs=(P("kown", "qown", None, None), P(), P(), P(), P(), P(), P()),
        out_specs=P("kown", "qown", None, None),
        check_vma=False,
    )
```

time: 3260 us -> 362 us (0.11)
  waiting for transfers between devices: 1330 us -> 138 us
  blocking collectives: 983 us -> 20 us
  local copies, waits for them, and re-layouts: 473 us -> 19.8 us
  matrix products: 245 us -> 0 us
  other arithmetic: 193 us -> 0 us
  Pallas kernels: 0 us -> 90.9 us
  starting transfers between devices: 19.7 us -> 91.1 us
    all_to_all x2 -> x3, waiting for transfers between devices: 1330 us -> 0.01 us  [add_x(): lax.all_to_all(summed[at], 'kown', split_axis=0, concat_axis=0, tiled=True)]
    all_to_all x2 -> x1, blocking collectives: 983 us -> 20 us  [add_x(): lax.all_to_all(summed[at], 'kown', split_axis=0, concat_axis=0, tiled=True)]
    dot_general x6 -> x0, matrix products: 245 us -> none  [the longest x1 58.2 us: transform_rows(): jnp.dot(sine_vals, flattened, preferred_element_type=jnp.float32)]
    all_to_all x6 -> x0, local copies, waits for them, and re-layouts: 239 us -> none  [the longest x2 124 us: per_device(): lax.all_to_all(arranged, 'qown', split_axis=0, concat_axis=1, tiled=True)]
    another operation x5 -> x0, other arithmetic: 170 us -> none
    ppermute x0 -> x36, waiting for transfers between devices: none -> 138 us  [swap(): return lax.ppermute(array, axis, [(i, i ^ bit) for i in range(size)])]
    pallas_call x0 -> x22, Pallas kernels: none -> 90.9 us  [the longest x4 37.6 us: interpolate(): pl.pallas_call(kernel, grid=(k_count // step,), in_specs=[pl.BlockSpec(we...]
    another operation x2 -> x0, local copies, waits for them, and re-layouts: 85.3 us -> none  [combine(): return jnp.stack([real_part, imag_part], axis=2)]
  transfers between devices with their start and end apart: 2 -> 39, of which waited for: 2 -> 15; matrix products, arithmetic and copies ran while one was open for 1% -> 0% of each run, Pallas kernels for 0% -> 13%
where the time goes in v1:
time: 362 us; the launch traced here: 360 us
  waiting for transfers between devices  138 us (38%)
  starting transfers between devices  91.1 us (25%)
  Pallas kernels  90.9 us (25%)
  blocking collectives  20 us (6%)
  local copies, waits for them, and re-layouts  19.8 us (5%)
    ppermute x36, waiting for transfers between devices, swap(): return lax.ppermute(array, axis, [(i, i ^ bit) for i in range(size)])  138 us
    ppermute x36, starting transfers between devices, swap(): return lax.ppermute(array, axis, [(i, i ^ bit) for i in range(size)])  72.8 us
    pallas_call x4, Pallas kernels, interpolate(): pl.pallas_call(kernel, grid=(k_count // step,), in_specs=[pl.BlockSpec(we...  37.6 us
    pallas_call x8, Pallas kernels, add(): pl.pallas_call(kernel, grid=(k_count // step,), in_specs=[part if array.n...  20.4 us
    all_to_all x1, blocking collectives, add_x(): lax.all_to_all(summed[at], 'kown', split_axis=0, concat_axis=0, tiled=True)  20 us
    unnamed x84, local copies, waits for them, and re-layouts  19.8 us
    all_to_all x3, starting transfers between devices, add_x(): lax.all_to_all(summed[at], 'kown', split_axis=0, concat_axis=0, tiled=True)  18.3 us
    pallas_call x4, Pallas kernels, to_cells(): pl.pallas_call(kernel, grid=(per_pair,), in_specs=[pl.BlockSpec(k_matrix....  15.8 us
  transfers between devices with their start and end apart: 39, of which 15 were waited for; matrix products, arithmetic and copies ran while one was open for 0% of the time, Pallas kernels for 13%

profile of v1, /device:TPU:8, one launch (start us, length us, event | category | flops | bytes accessed | tf_op | source)
XLA Modules:
  0.0 359.8 jit_solution(14812219816292768368)
XLA Ops:
  4.4 6.8 %interpolate.4 = (bf16[2,8,2,64,2,128]{5,4,3,2,1,0:T(2,128)(2,1)S(1)}, bf16[2,8,2,64,2,128]{5,4,3,2,1,0:T(2,128)(2,1)S(1)}) custom-call(bf16[128,256]{1,0:T(8,128)(2,1)S(1)} %fine_weights.1.w_ref, bf16[64,128,2,1280]{3,2,1,0:T(2,128)(2,1)} %g_ref.7), custom_call_target="tpu_custom_call" | custom-call | tf_op jit(solution)/shard_map/interpolate/pallas_call | solution.py:123
  11.3 10.0 %interpolate.5 = (bf16[2,8,2,64,2,384]{5,4,3,2,1,0:T(2,128)(2,1)S(1)}, bf16[2,8,2,64,2,384]{5,4,3,2,1,0:T(2,128)(2,1)S(1)}) custom-call(bf16[128,256]{1,0:T(8,128)(2,1)S(1)} %fine_weights.1.w_ref, bf16[64,128,2,1280]{3,2,1,0:T(2,128)(2,1)} %g_ref.7), custom_call_target="tpu_custom_call" | custom-call | tf_op jit(solution)/shard_map/interpolate/pallas_call | solution.py:123
  21.9 6.6 %collective-permute-done.refs_1_ = bf16[2,8,2,64,2,128]{5,4,3,2,1,0:T(2,128)(2,1)S(1)} collective-permute-done((bf16[2,8,2,64,2,128]{5,4,3,2,1,0:T(2,128)(2,1)S(1)}, bf16[2,8,2,64,2,128]{5,4,3,2,1,0:T(2,128)(2,1)S(1)}, u32[]{:S(2)}, u32[]{:S(2)}) %collective-permute-start) | collective-permute-done | bytes 1048608 | tf_op jit(solution)/shard_map/ppermute | solution.py:217
  31.1 5.4 %k_phases.1.m_ref = bf16[1024,1024]{1,0:T(8,128)(2,1)S(1)} custom-call(s32[3,512]{1,0:T(4,128)S(1)} %copy-done.28, s32[3,512]{1,0:T(4,128)S(1)} %copy-done.29), custom_call_target="tpu_custom_call" | custom-call | tf_op jit(solution)/shard_map/k_phases/pallas_call | solution.py:97
  38.8 4.8 %collective-permute-done.2.refs_2_ = bf16[8,2,64,2,128]{4,3,2,1,0:T(2,128)(2,1)S(1)} collective-permute-done((bf16[8,2,64,2,128]{4,3,2,1,0:T(2,128)(2,1)S(1)}, bf16[8,2,64,2,128]{4,3,2,1,0:T(2,128)(2,1)S(1)}, u32[]{:S(2)}, u32[]{:S(2)}) %collective-permute-start.2) | collective-permute-done | bytes 524320 | tf_op jit(solution)/shard_map/ppermute | solution.py:217
  44.9 10.0 %interpolate.6 = (bf16[2,8,2,64,2,384]{5,4,3,2,1,0:T(2,128)(2,1)S(1)}, bf16[2,8,2,64,2,384]{5,4,3,2,1,0:T(2,128)(2,1)S(1)}) custom-call(bf16[128,256]{1,0:T(8,128)(2,1)S(1)} %fine_weights.1.w_ref, bf16[64,128,2,1280]{3,2,1,0:T(2,128)(2,1)} %g_ref.7), custom_call_target="tpu_custom_call" | custom-call | tf_op jit(solution)/shard_map/interpolate/pallas_call | solution.py:123
  56.6 20.0 %all_to_all.20.in_ref = bf16[8,2,64,2,128]{4,3,2,1,0:T(2,128)(2,1)S(1)} all-to-all(bf16[8,2,64,2,128]{4,3,2,1,0:T(2,128)(2,1)S(1)} %add_x.4), channel_id=1, replica_groups=mesh['kown'=8,'qown'=4] {'kown'}, dimensions={0} | all-to-all | bytes 1048576 | tf_op jit(solution)/shard_map/all_to_all | solution.py:265
  82.1 9.7 %collective-permute-done.3.refs_2_ = bf16[8,2,64,2,384]{4,3,2,1,0:T(2,128)(2,1)S(1)} collective-permute-done((bf16[8,2,64,2,384]{4,3,2,1,0:T(2,128)(2,1)S(1)}, bf16[8,2,64,2,384]{4,3,2,1,0:T(2,128)(2,1)S(1)}, u32[]{:S(2)}, u32[]{:S(2)}) %collective-permute-start.3) | collective-permute-done | bytes 1572896 | tf_op jit(solution)/shard_map/ppermute | solution.py:217
  95.9 10.7 %interpolate.7 = (bf16[2,8,2,64,2,384]{5,4,3,2,1,0:T(2,128)(2,1)S(1)}, bf16[2,8,2,64,2,384]{5,4,3,2,1,0:T(2,128)(2,1)}) custom-call(bf16[128,256]{1,0:T(8,128)(2,1)S(1)} %fine_weights.1.w_ref, bf16[64,128,2,1280]{3,2,1,0:T(2,128)(2,1)} %g_ref.7), custom_call_target="tpu_custom_call" | custom-call | tf_op jit(solution)/shard_map/interpolate/pallas_call | solution.py:123
  108.3 6.3 %all-to-all-start.1 = ((bf16[8,2,64,2,384]{4,3,2,1,0:T(2,128)(2,1)}), bf16[8,2,64,2,384]{4,3,2,1,0:T(2,128)(2,1)}, u32[]{:S(2)}, u32[]{:S(2)}) async-start(bf16[8,2,64,2,384]{4,3,2,1,0:T(2,128)(2,1)} %copy-done.9), calls=%async_computation.1 | async-start | bytes 3145728 | tf_op jit(solution)/shard_map/all_to_all | solution.py:265
  123.0 28.1 %collective-permute-done.14.refs_2_ = bf16[8,2,64,2,384]{4,3,2,1,0:T(2,128)(2,1)S(1)} collective-permute-done((bf16[8,2,64,2,384]{4,3,2,1,0:T(2,128)(2,1)}, bf16[8,2,64,2,384]{4,3,2,1,0:T(2,128)(2,1)S(1)}, u32[]{:S(2)}, u32[]{:S(2)}) %collective-permute-start.14) | collective-permute-done | bytes 1572896 | tf_op jit(solution)/shard_map/ppermute | solution.py:217
  155.1 6.0 %all-to-all-start.3 = ((bf16[8,2,64,2,384]{4,3,2,1,0:T(2,128)(2,1)}), bf16[8,2,64,2,384]{4,3,2,1,0:T(2,128)(2,1)}, u32[]{:S(2)}, u32[]{:S(2)}) async-start(bf16[8,2,64,2,384]{4,3,2,1,0:T(2,128)(2,1)} %copy-done.8), calls=%async_computation.3 | async-start | bytes 3145728 | tf_op jit(solution)/shard_map/all_to_all | solution.py:265
  162.6 4.7 %to_cells.5 = (bf16[64,2,2,384]{3,2,1,0:T(2,128)(2,1)S(1)}, bf16[64,2,2,384]{3,2,1,0:T(2,128)(2,1)S(1)}, bf16[64,2,2,384]{3,2,1,0:T(2,128)(2,1)}, bf16[64,2,2,38...) custom-call(bf16[1024,1024]{1,0:T(8,128)(2,1)S(1)} %k_phases.1.m_ref, ...), custom_call_target="tpu_custom_call" | custom-call | tf_op jit(solution)/shard_map/to_cells/pallas_call | solution.py:174
  168.1 28.1 %collective-permute-done.6.refs_2_ = bf16[8,2,64,2,384]{4,3,2,1,0:T(2,128)(2,1)S(1)} collective-permute-done((bf16[8,2,64,2,384]{4,3,2,1,0:T(2,128)(2,1)}, bf16[8,2,64,2,384]{4,3,2,1,0:T(2,128)(2,1)S(1)}, u32[]{:S(2)}, u32[]{:S(2)}) %collective-permute-start.6) | collective-permute-done | bytes 1572896 | tf_op jit(solution)/shard_map/ppermute | solution.py:217
  201.1 6.0 %all-to-all-start.2 = ((bf16[8,2,64,2,384]{4,3,2,1,0:T(2,128)(2,1)}), bf16[8,2,64,2,384]{4,3,2,1,0:T(2,128)(2,1)}, u32[]{:S(2)}, u32[]{:S(2)}) async-start(bf16[8,2,64,2,384]{4,3,2,1,0:T(2,128)(2,1)} %copy-done.7), calls=%async_computation.2 | async-start | bytes 3145728 | tf_op jit(solution)/shard_map/all_to_all | solution.py:265
  214.4 10.8 %collective-permute-done.29.refs_1_ = bf16[64,2,2,128]{3,2,1,0:T(2,128)(2,1)S(1)} collective-permute-done((bf16[64,2,2,128]{3,2,1,0:T(2,128)(2,1)S(1)}, bf16[64,2,2,128]{3,2,1,0:T(2,128)(2,1)S(1)}, u32[]{:S(2)}, u32[]{:S(2)}) %collective-permute-start.29) | collective-permute-done | bytes 65568 | tf_op jit(solution)/shard_map/ppermute | solution.py:217
  225.9 6.0 %collective-permute-start.33 = (bf16[64,2,2,128]{3,2,1,0:T(2,128)(2,1)S(1)}, bf16[64,2,2,128]{3,2,1,0:T(2,128)(2,1)S(1)}, u32[]{:S(2)}, u32[]{:S(2)}) collective-permute-start(bf16[64,2,2,128]{3,2,1,0:T(2,128)(2,1)S(1)} %get-tuple-element.122), channel_id=1, source_target_pairs={{0,20},{4,16},{8,28},{12,24},{16,4},{20,0},{24,12},{28,8},{1,21},{... | collective-permute-start | bytes 196616 | tf_op jit(solution)/shard_map/ppermute | solution.py:217
  241.5 5.4 %collective-permute-done.32.refs_4_ = bf16[64,2,2,128]{3,2,1,0:T(2,128)(2,1)S(1)} collective-permute-done((bf16[64,2,2,128]{3,2,1,0:T(2,128)(2,1)S(1)}, bf16[64,2,2,128]{3,2,1,0:T(2,128)(2,1)S(1)}, u32[]{:S(2)}, u32[]{:S(2)}) %collective-permute-start.32) | collective-permute-done | bytes 65568 | tf_op jit(solution)/shard_map/ppermute | solution.py:217
  273.5 7.4 %collective-permute-start.16 = (bf16[64,2,2,384]{3,2,1,0:T(2,128)(2,1)}, bf16[64,2,2,384]{3,2,1,0:T(2,128)(2,1)}, u32[]{:S(2)}, u32[]{:S(2)}) collective-permute-start(bf16[64,2,2,384]{3,2,1,0:T(2,128)(2,1)} %get-tuple-element.103), channel_id=1, source_target_pairs={{0,8},{4,12},{8,0},{12,4},{16,24},{20,28},{24,16},{28,20},{1,9},{5... | collective-permute-start | bytes 589832 | tf_op jit(solution)/shard_map/ppermute | solution.py:217
  280.8 5.1 %collective-permute-start.17 = (bf16[64,2,2,384]{3,2,1,0:T(2,128)(2,1)}, bf16[64,2,2,384]{3,2,1,0:T(2,128)(2,1)}, u32[]{:S(2)}, u32[]{:S(2)}) collective-permute-start(bf16[64,2,2,384]{3,2,1,0:T(2,128)(2,1)} %get-tuple-element.104), channel_id=1, source_target_pairs={{0,12},{4,8},{8,4},{12,0},{16,28},{20,24},{24,20},{28,16},{1,13},{... | collective-permute-start | bytes 589832 | tf_op jit(solution)/shard_map/ppermute | solution.py:217
  293.5 8.7 %collective-permute-done.28.refs_7_ = bf16[64,2,2,384]{3,2,1,0:T(2,128)(2,1)} collective-permute-done((bf16[64,2,2,384]{3,2,1,0:T(2,128)(2,1)}, bf16[64,2,2,384]{3,2,1,0:T(2,128)(2,1)}, u32[]{:S(2)}, u32[]{:S(2)}) %collective-permute-start.28) | collective-permute-done | bytes 196640 | tf_op jit(solution)/shard_map/ppermute | solution.py:217
  307.2 11.1 %collective-permute-done.19.refs_5_ = bf16[64,2,2,384]{3,2,1,0:T(2,128)(2,1)S(1)} collective-permute-done((bf16[64,2,2,384]{3,2,1,0:T(2,128)(2,1)S(1)}, bf16[64,2,2,384]{3,2,1,0:T(2,128)(2,1)S(1)}, u32[]{:S(2)}, u32[]{:S(2)}) %collective-permute-start.19) | collective-permute-done | bytes 196640 | tf_op jit(solution)/shard_map/ppermute | solution.py:217
  325.8 6.8 %collective-permute-done.21.refs_7_ = bf16[64,2,2,384]{3,2,1,0:T(2,128)(2,1)S(1)} collective-permute-done((bf16[64,2,2,384]{3,2,1,0:T(2,128)(2,1)S(1)}, bf16[64,2,2,384]{3,2,1,0:T(2,128)(2,1)S(1)}, u32[]{:S(2)}, u32[]{:S(2)}) %collective-permute-start.21) | collective-permute-done | bytes 196640 | tf_op jit(solution)/shard_map/ppermute | solution.py:217
  332.5 10.7 %collective-permute-start.11 = (bf16[64,2,2,384]{3,2,1,0:T(2,128)(2,1)S(1)}, bf16[64,2,2,384]{3,2,1,0:T(2,128)(2,1)S(1)}, u32[]{:S(2)}, u32[]{:S(2)}) collective-permute-start(bf16[64,2,2,384]{3,2,1,0:T(2,128)(2,1)S(1)} %get-tuple-element.96), channel_id=1, source_target_pairs={{0,20},{4,16},{8,28},{12,24},{16,4},{20,0},{24,12},{28,8},{1,21},{... | collective-permute-start | bytes 589832 | tf_op jit(solution)/shard_map/ppermute | solution.py:217
  (161 shorter events, 124.1 us)
Async XLA Ops:
  55.0 23.6 %collective-permute-start.4 = (bf16[2,8,2,64,2,384]{5,4,3,2,1,0:T(2,128)(2,1)S(1)}, bf16[2,8,2,64,2,384]{5,4,3,2,1,0:T(2,128)(2,1)S(1)}, u32[]{:S(2)}, u32[]{:S(2)}) collective-permute-start(bf16[2,8,2,64,2,384]{5,4,3,2,1,0:T(2,128)(2,1)S(1)} %get-tuple-element.80), channel_id=1, source_target_pairs={{0,1},{1,0},{2,3},{3,2},{4,5},{5,4},{6,7},{7,6},{8,9},{9,8},{10,11... | collective-permute-start | bytes 9437192 | tf_op jit(solution)/shard_map/ppermute | solution.py:217
  55.0 36.8 %collective-permute-start.3 = (bf16[8,2,64,2,384]{4,3,2,1,0:T(2,128)(2,1)S(1)}, bf16[8,2,64,2,384]{4,3,2,1,0:T(2,128)(2,1)S(1)}, u32[]{:S(2)}, u32[]{:S(2)}) collective-permute-start(bf16[8,2,64,2,384]{4,3,2,1,0:T(2,128)(2,1)S(1)} %add_core.5), channel_id=1, source_target_pairs={{0,2},{1,3},{2,0},{3,1},{4,6},{5,7},{6,4},{7,5},{8,10},{9,11},{10,... | collective-permute-start | bytes 4718600 | tf_op jit(solution)/shard_map/ppermute | solution.py:217
  108.3 46.8 %all-to-all-start.1 = ((bf16[8,2,64,2,384]{4,3,2,1,0:T(2,128)(2,1)}), bf16[8,2,64,2,384]{4,3,2,1,0:T(2,128)(2,1)}, u32[]{:S(2)}, u32[]{:S(2)}) async-start(bf16[8,2,64,2,384]{4,3,2,1,0:T(2,128)(2,1)} %copy-done.9), calls=%async_computation.1 | async-start | bytes 3145728 | tf_op jit(solution)/shard_map/all_to_all | solution.py:265
  114.6 36.5 %collective-permute-start.14 = (bf16[8,2,64,2,384]{4,3,2,1,0:T(2,128)(2,1)}, bf16[8,2,64,2,384]{4,3,2,1,0:T(2,128)(2,1)S(1)}, u32[]{:S(2)}, u32[]{:S(2)}) collective-permute-start(bf16[8,2,64,2,384]{4,3,2,1,0:T(2,128)(2,1)} %copy-done.11), channel_id=1, source_target_pairs={{0,2},{1,3},{2,0},{3,1},{4,6},{5,7},{6,4},{7,5},{8,10},{9,11},{10,... | collective-permute-start | bytes 4718600 | tf_op jit(solution)/shard_map/ppermute | solution.py:217
  155.1 46.0 %all-to-all-start.3 = ((bf16[8,2,64,2,384]{4,3,2,1,0:T(2,128)(2,1)}), bf16[8,2,64,2,384]{4,3,2,1,0:T(2,128)(2,1)}, u32[]{:S(2)}, u32[]{:S(2)}) async-start(bf16[8,2,64,2,384]{4,3,2,1,0:T(2,128)(2,1)} %copy-done.8), calls=%async_computation.3 | async-start | bytes 3145728 | tf_op jit(solution)/shard_map/all_to_all | solution.py:265
  161.1 35.0 %collective-permute-start.6 = (bf16[8,2,64,2,384]{4,3,2,1,0:T(2,128)(2,1)}, bf16[8,2,64,2,384]{4,3,2,1,0:T(2,128)(2,1)S(1)}, u32[]{:S(2)}, u32[]{:S(2)}) collective-permute-start(bf16[8,2,64,2,384]{4,3,2,1,0:T(2,128)(2,1)} %copy-done.10), channel_id=1, source_target_pairs={{0,2},{1,3},{2,0},{3,1},{4,6},{5,7},{6,4},{7,5},{8,10},{9,11},{10,... | collective-permute-start | bytes 4718600 | tf_op jit(solution)/shard_map/ppermute | solution.py:217
  201.1 87.9 %all-to-all-start.2 = ((bf16[8,2,64,2,384]{4,3,2,1,0:T(2,128)(2,1)}), bf16[8,2,64,2,384]{4,3,2,1,0:T(2,128)(2,1)}, u32[]{:S(2)}, u32[]{:S(2)}) async-start(bf16[8,2,64,2,384]{4,3,2,1,0:T(2,128)(2,1)} %copy-done.7), calls=%async_computation.2 | async-start | bytes 3145728 | tf_op jit(solution)/shard_map/all_to_all | solution.py:265
  207.1 51.4 %collective-permute-start.22 = (bf16[64,2,2,384]{3,2,1,0:T(2,128)(2,1)S(1)}, bf16[64,2,2,384]{3,2,1,0:T(2,128)(2,1)S(1)}, u32[]{:S(2)}, u32[]{:S(2)}) collective-permute-start(bf16[64,2,2,384]{3,2,1,0:T(2,128)(2,1)S(1)} %get-tuple-element.110), channel_id=1, source_target_pairs={{0,4},{4,0},{8,12},{12,8},{16,20},{20,16},{24,28},{28,24},{1,5},{5... | collective-permute-start | bytes 589832 | tf_op jit(solution)/shard_map/ppermute | solution.py:217
  209.1 26.2 %collective-permute-start.30 = (bf16[64,2,2,128]{3,2,1,0:T(2,128)(2,1)S(1)}, bf16[64,2,2,128]{3,2,1,0:T(2,128)(2,1)S(1)}, u32[]{:S(2)}, u32[]{:S(2)}) collective-permute-start(bf16[64,2,2,128]{3,2,1,0:T(2,128)(2,1)S(1)} %get-tuple-element.119), channel_id=1, source_target_pairs={{0,8},{4,12},{8,0},{12,4},{16,24},{20,28},{24,16},{28,20},{1,9},{5... | collective-permute-start | bytes 196616 | tf_op jit(solution)/shard_map/ppermute | solution.py:217
  209.2 30.0 %collective-permute-start.31 = (bf16[64,2,2,128]{3,2,1,0:T(2,128)(2,1)S(1)}, bf16[64,2,2,128]{3,2,1,0:T(2,128)(2,1)S(1)}, u32[]{:S(2)}, u32[]{:S(2)}) collective-permute-start(bf16[64,2,2,128]{3,2,1,0:T(2,128)(2,1)S(1)} %get-tuple-element.120), channel_id=1, source_target_pairs={{0,12},{4,8},{8,4},{12,0},{16,28},{20,24},{24,20},{28,16},{1,13},{... | collective-permute-start | bytes 196616 | tf_op jit(solution)/shard_map/ppermute | solution.py:217
  212.1 34.8 %collective-permute-start.32 = (bf16[64,2,2,128]{3,2,1,0:T(2,128)(2,1)S(1)}, bf16[64,2,2,128]{3,2,1,0:T(2,128)(2,1)S(1)}, u32[]{:S(2)}, u32[]{:S(2)}) collective-permute-start(bf16[64,2,2,128]{3,2,1,0:T(2,128)(2,1)S(1)} %get-tuple-element.121), channel_id=1, source_target_pairs={{0,16},{4,20},{8,24},{12,28},{16,0},{20,4},{24,8},{28,12},{1,17},{... | collective-permute-start | bytes 196616 | tf_op jit(solution)/shard_map/ppermute | solution.py:217
  225.9 26.2 %collective-permute-start.33 = (bf16[64,2,2,128]{3,2,1,0:T(2,128)(2,1)S(1)}, bf16[64,2,2,128]{3,2,1,0:T(2,128)(2,1)S(1)}, u32[]{:S(2)}, u32[]{:S(2)}) collective-permute-start(bf16[64,2,2,128]{3,2,1,0:T(2,128)(2,1)S(1)} %get-tuple-element.122), channel_id=1, source_target_pairs={{0,20},{4,16},{8,28},{12,24},{16,4},{20,0},{24,12},{28,8},{1,21},{... | collective-permute-start | bytes 196616 | tf_op jit(solution)/shard_map/ppermute | solution.py:217
  254.9 25.9 %collective-permute-start.26 = (bf16[64,2,2,384]{3,2,1,0:T(2,128)(2,1)}, bf16[64,2,2,384]{3,2,1,0:T(2,128)(2,1)S(1)}, u32[]{:S(2)}, u32[]{:S(2)}) collective-permute-start(bf16[64,2,2,384]{3,2,1,0:T(2,128)(2,1)} %get-tuple-element.114), channel_id=1, source_target_pairs={{0,20},{4,16},{8,28},{12,24},{16,4},{20,0},{24,12},{28,8},{1,21},{... | collective-permute-start | bytes 589832 | tf_op jit(solution)/shard_map/ppermute | solution.py:217
  258.5 30.5 %collective-permute-start.27 = (bf16[64,2,2,384]{3,2,1,0:T(2,128)(2,1)}, bf16[64,2,2,384]{3,2,1,0:T(2,128)(2,1)S(1)}, u32[]{:S(2)}, u32[]{:S(2)}) collective-permute-start(bf16[64,2,2,384]{3,2,1,0:T(2,128)(2,1)} %copy-done.35), channel_id=1, source_target_pairs={{0,24},{4,28},{8,16},{12,20},{16,8},{20,12},{24,0},{28,4},{1,25},{... | collective-permute-start | bytes 589832 | tf_op jit(solution)/shard_map/ppermute | solution.py:217
  266.0 36.3 %collective-permute-start.28 = (bf16[64,2,2,384]{3,2,1,0:T(2,128)(2,1)}, bf16[64,2,2,384]{3,2,1,0:T(2,128)(2,1)}, u32[]{:S(2)}, u32[]{:S(2)}) collective-permute-start(bf16[64,2,2,384]{3,2,1,0:T(2,128)(2,1)} %copy-done.34), channel_id=1, source_target_pairs={{0,28},{4,24},{8,20},{12,16},{16,12},{20,8},{24,4},{28,0},{1,29},{... | collective-permute-start | bytes 589832 | tf_op jit(solution)/shard_map/ppermute | solution.py:217
  268.2 34.0 %collective-permute-start.15 = (bf16[64,2,2,384]{3,2,1,0:T(2,128)(2,1)}, bf16[64,2,2,384]{3,2,1,0:T(2,128)(2,1)}, u32[]{:S(2)}, u32[]{:S(2)}) collective-permute-start(bf16[64,2,2,384]{3,2,1,0:T(2,128)(2,1)} %get-tuple-element.102), channel_id=1, source_target_pairs={{0,4},{4,0},{8,12},{12,8},{16,20},{20,16},{24,28},{28,24},{1,5},{5... | collective-permute-start | bytes 589832 | tf_op jit(solution)/shard_map/ppermute | solution.py:217
  273.5 28.8 %collective-permute-start.16 = (bf16[64,2,2,384]{3,2,1,0:T(2,128)(2,1)}, bf16[64,2,2,384]{3,2,1,0:T(2,128)(2,1)}, u32[]{:S(2)}, u32[]{:S(2)}) collective-permute-start(bf16[64,2,2,384]{3,2,1,0:T(2,128)(2,1)} %get-tuple-element.103), channel_id=1, source_target_pairs={{0,8},{4,12},{8,0},{12,4},{16,24},{20,28},{24,16},{28,20},{1,9},{5... | collective-permute-start | bytes 589832 | tf_op jit(solution)/shard_map/ppermute | solution.py:217
  280.8 24.8 %collective-permute-start.17 = (bf16[64,2,2,384]{3,2,1,0:T(2,128)(2,1)}, bf16[64,2,2,384]{3,2,1,0:T(2,128)(2,1)}, u32[]{:S(2)}, u32[]{:S(2)}) collective-permute-start(bf16[64,2,2,384]{3,2,1,0:T(2,128)(2,1)} %get-tuple-element.104), channel_id=1, source_target_pairs={{0,12},{4,8},{8,4},{12,0},{16,28},{20,24},{24,20},{28,16},{1,13},{... | collective-permute-start | bytes 589832 | tf_op jit(solution)/shard_map/ppermute | solution.py:217
  302.2 23.5 %collective-permute-start.20 = (bf16[64,2,2,384]{3,2,1,0:T(2,128)(2,1)S(1)}, bf16[64,2,2,384]{3,2,1,0:T(2,128)(2,1)S(1)}, u32[]{:S(2)}, u32[]{:S(2)}) collective-permute-start(bf16[64,2,2,384]{3,2,1,0:T(2,128)(2,1)S(1)} %copy-done.39), channel_id=1, source_target_pairs={{0,24},{4,28},{8,16},{12,20},{16,8},{20,12},{24,0},{28,4},{1,25},{... | collective-permute-start | bytes 589832 | tf_op jit(solution)/shard_map/ppermute | solution.py:217
  302.3 30.2 %collective-permute-start.21 = (bf16[64,2,2,384]{3,2,1,0:T(2,128)(2,1)S(1)}, bf16[64,2,2,384]{3,2,1,0:T(2,128)(2,1)S(1)}, u32[]{:S(2)}, u32[]{:S(2)}) collective-permute-start(bf16[64,2,2,384]{3,2,1,0:T(2,128)(2,1)S(1)} %copy-done.37), channel_id=1, source_target_pairs={{0,28},{4,24},{8,20},{12,16},{16,12},{20,8},{24,4},{28,0},{1,29},{... | collective-permute-start | bytes 589832 | tf_op jit(solution)/shard_map/ppermute | solution.py:217
  305.7 26.8 %collective-permute-start.7 = (bf16[64,2,2,384]{3,2,1,0:T(2,128)(2,1)S(1)}, bf16[64,2,2,384]{3,2,1,0:T(2,128)(2,1)S(1)}, u32[]{:S(2)}, u32[]{:S(2)}) collective-permute-start(bf16[64,2,2,384]{3,2,1,0:T(2,128)(2,1)S(1)} %get-tuple-element.92), channel_id=1, source_target_pairs={{0,4},{4,0},{8,12},{12,8},{16,20},{20,16},{24,28},{28,24},{1,5},{5... | collective-permute-start | bytes 589832 | tf_op jit(solution)/shard_map/ppermute | solution.py:217
  305.8 37.4 %collective-permute-start.13 = (bf16[64,2,2,384]{3,2,1,0:T(2,128)(2,1)S(1)}, bf16[64,2,2,384]{3,2,1,0:T(2,128)(2,1)S(1)}, u32[]{:S(2)}, u32[]{:S(2)}) collective-permute-start(bf16[64,2,2,384]{3,2,1,0:T(2,128)(2,1)S(1)} %get-tuple-element.98), channel_id=1, source_target_pairs={{0,28},{4,24},{8,20},{12,16},{16,12},{20,8},{24,4},{28,0},{1,29},{... | collective-permute-start | bytes 589832 | tf_op jit(solution)/shard_map/ppermute | solution.py:217
  318.3 36.1 %collective-permute-start.8 = (bf16[64,2,2,384]{3,2,1,0:T(2,128)(2,1)S(1)}, bf16[64,2,2,384]{3,2,1,0:T(2,128)(2,1)S(1)}, u32[]{:S(2)}, u32[]{:S(2)}) collective-permute-start(bf16[64,2,2,384]{3,2,1,0:T(2,128)(2,1)S(1)} %get-tuple-element.93), channel_id=1, source_target_pairs={{0,8},{4,12},{8,0},{12,4},{16,24},{20,28},{24,16},{28,20},{1,9},{5... | collective-permute-start | bytes 589832 | tf_op jit(solution)/shard_map/ppermute | solution.py:217
  325.8 28.7 %collective-permute-start.9 = (bf16[64,2,2,384]{3,2,1,0:T(2,128)(2,1)S(1)}, bf16[64,2,2,384]{3,2,1,0:T(2,128)(2,1)S(1)}, u32[]{:S(2)}, u32[]{:S(2)}) collective-permute-start(bf16[64,2,2,384]{3,2,1,0:T(2,128)(2,1)S(1)} %get-tuple-element.94), channel_id=1, source_target_pairs={{0,12},{4,8},{8,4},{12,0},{16,28},{20,24},{24,20},{28,16},{1,13},{... | collective-permute-start | bytes 589832 | tf_op jit(solution)/shard_map/ppermute | solution.py:217
  (57 other events, 900.4 us)

commit v2 on v1

--- a/solution.py
+++ b/solution.py
@@ -46,18 +46,13 @@
     q_count = q_total // qown if near else q_total
 
     def kernel(f_ref, rp_ref, degen_ref, q_ref, out_ref):
-        first = lax.axis_index("qown") * q_count if near else 0
-        block = f_total // qown
-
-        def fine_index(n):
-            if not near:
-                return n >> 1
-            owner = n // (2 * block)
-            owner = ((owner & 1) * (qown // 2) + (owner >> 1)) ^ lax.axis_index("qown")
-            return owner * block + ((n >> 1) & (block - 1))
-
+        mask, first = 0, 0
+        if near:
+            me_k, me_q = lax.axis_index("kown"), lax.axis_index("qown")
+            mask = (me_q * kown + me_k) * (f_total // (qown * kown))
+            first = me_q * q_count
         rp = rp_ref[...].astype(F32).astype(BF16)
-        fine = spread(f_ref[...], 2 * f_total, fine_index)
+        fine = spread(f_ref[...], 2 * f_total, lambda n: (n >> 1) ^ mask)
         q_near = spread(q_ref[...], 2 * q_count, lambda n: (n >> 1) + first)
         f_turns = products(fine, rp)
         q_turns = products(rp, q_near)
@@ -87,7 +82,7 @@
 
         @pl.when(at == 0)
         def _():
-            columns[...] = spread(k_ref[...], 2 * points, lambda n: n >> 1)
+            columns[...] = spread(k_ref[...], 2 * points, lambda n: (n >> 1) ^ (me_k * (points // kown)))
 
         row = spread(re_ref[...], rows, lambda n: (n >> 1) + (at ^ me_k) * (cells // kown))
         turns = products(row, columns[...])
@@ -106,20 +101,20 @@
     )(re_cells, k_points)
 
 
-def interpolate(weights, g, start, width, pairs, per_pair):
+def interpolate(weights, g, start, width, parts, pairs, per_pair):
     k_count, q_count = g.shape[:2]
     step = 8
-    half = weights.shape[0] // 2
+    rows = pairs * per_pair * 2
 
     def kernel(w_ref, g_ref, *out_refs):
         for at in range(step):
             operand = g_ref[at].reshape(2 * q_count, width)
             product = jnp.dot(w_ref[...], operand, preferred_element_type=F32).astype(BF16)
-            for core in range(2):
-                block = product[core * half : (core + 1) * half]
-                out_refs[core][:, :, :, at] = block.reshape(2, pairs, per_pair, 2, width)
-
-    shape = jax.ShapeDtypeStruct((2, pairs, per_pair, k_count, 2, width), BF16)
+            for part in range(parts):
+                block = product[part * rows : (part + 1) * rows]
+                out_refs[part][:, :, at] = block.reshape(pairs, per_pair, 2, width)
+
+    shape = jax.ShapeDtypeStruct((pairs, per_pair, k_count, 2, width), BF16)
     return pl.pallas_call(
         kernel,
         grid=(k_count // step,),
@@ -130,59 +125,79 @@
                 lambda i: (i * step, 0, 0, start),
             ),
         ],
-        out_specs=[pl.BlockSpec((2, pairs, per_pair, step, 2, width), lambda i: (0, 0, 0, i, 0, 0))] * 2,
-        out_shape=[shape] * 2,
+        out_specs=[pl.BlockSpec((pairs, per_pair, step, 2, width), lambda i: (0, 0, i, 0, 0))] * parts,
+        out_shape=[shape] * parts,
         compiler_params=pltpu.CompilerParams(vmem_limit_bytes=12 << 20),
         name="interpolate",
     )(weights, g)
 
 
-def add(name, which, *arrays):
-    pairs, per_pair, k_count, _, width = arrays[0].shape[-5:]
+def add_two(former, latter):
+    pairs, per_pair, k_count, _, width = former.shape
     step = 16
 
-    def kernel(*refs):
+    def kernel(a_ref, b_ref, out_ref):
         for pair in range(pairs):
             for j in range(per_pair):
-                total = sum(ref[pair, j].reshape(2 * step, width).astype(F32) for ref in refs[:-1])
-                refs[-1][pair, j] = total.astype(BF16).reshape(step, 2, width)
-
-    block = (pairs, per_pair, step, 2, width)
-    whole = pl.BlockSpec(block, lambda i: (0, 0, i, 0, 0))
-    part = pl.BlockSpec((pl.Squeezed(),) + block, lambda i: (which, 0, 0, i, 0, 0))
+                a, b = (ref[pair, j].reshape(2 * step, width).astype(F32) for ref in (a_ref, b_ref))
+                out_ref[pair, j] = (a + b).astype(BF16).reshape(step, 2, width)
+
+    spec = pl.BlockSpec((pairs, per_pair, step, 2, width), lambda i: (0, 0, i, 0, 0))
     return pl.pallas_call(
         kernel,
         grid=(k_count // step,),
-        in_specs=[part if array.ndim == 6 else whole for array in arrays],
-        out_specs=whole,
-        out_shape=jax.ShapeDtypeStruct(arrays[0].shape[-5:], BF16),
+        in_specs=[spec] * 2,
+        out_specs=spec,
+        out_shape=jax.ShapeDtypeStruct(former.shape, BF16),
         compiler_params=pltpu.CompilerParams(vmem_limit_bytes=8 << 20),
-        name=name,
-    )(*arrays)
-
-
-def to_cells(k_matrix, rows):
-    owners, per_pair, k_count, _, width = rows.shape
-
-    def kernel(m_ref, in_ref, *out_refs):
-        operand = in_ref[:, 0].reshape(owners * 2 * k_count, width)
-        for at in range(owners):
-            part = m_ref[at * 2 * k_count : (at + 1) * 2 * k_count, :]
-            product = jnp.dot(part, operand, preferred_element_type=F32).astype(BF16)
-            out_refs[at][:, 0] = product.reshape(k_count, 2, width)
+        name="add_two",
+    )(former, latter)
+
+
+def add_split(one, two, three):
+    pairs, per_pair, k_count, _, width = one.shape
+    step = 16
+
+    def kernel(a_ref, b_ref, c_ref, *out_refs):
+        for pair in range(pairs):
+            for j in range(per_pair):
+                a, b, c = (ref[pair, j].reshape(2 * step, width).astype(F32) for ref in (a_ref, b_ref, c_ref))
+                out_refs[pair][j] = (a + b + c).astype(BF16).reshape(step, 2, width)
+
+    spec = pl.BlockSpec((pairs, per_pair, step, 2, width), lambda i: (0, 0, i, 0, 0))
+    return pl.pallas_call(
+        kernel,
+        grid=(k_count // step,),
+        in_specs=[spec] * 3,
+        out_specs=[pl.BlockSpec((per_pair, step, 2, width), lambda i: (0, i, 0, 0))] * pairs,
+        out_shape=[jax.ShapeDtypeStruct((per_pair, k_count, 2, width), BF16)] * pairs,
+        compiler_params=pltpu.CompilerParams(vmem_limit_bytes=8 << 20),
+        name="add_split",
+    )(one, two, three)
+
+
+def to_cells(k_matrix, blocks):
+    per_pair, k_count, _, width = blocks[0].shape
+    count = len(blocks)
+
+    def kernel(m_ref, *refs):
+        ins, outs = refs[:count], refs[count:]
+        operand = jnp.concatenate([ref[0].reshape(2 * k_count, width) for ref in ins], axis=0)
+        for at in range(count):
+            rows = m_ref[at * 2 * k_count : (at + 1) * 2 * k_count, :]
+            product = jnp.dot(rows, operand, preferred_element_type=F32).astype(BF16)
+            outs[at][:, 0] = product.reshape(k_count, 2, width)
 
     return pl.pallas_call(
         kernel,
         grid=(per_pair,),
-        in_specs=[
-            pl.BlockSpec(k_matrix.shape, lambda j: (0, 0)),
-            pl.BlockSpec((owners, 1, k_count, 2, width), lambda j: (0, j, 0, 0, 0)),
-        ],
-        out_specs=[pl.BlockSpec((k_count, 1, 2, width), lambda j: (0, j, 0, 0))] * owners,
-        out_shape=[jax.ShapeDtypeStruct((k_count, per_pair, 2, width), BF16)] * owners,
+        in_specs=[pl.BlockSpec(k_matrix.shape, lambda j: (0, 0))]
+        + [pl.BlockSpec((1, k_count, 2, width), lambda j: (j, 0, 0, 0))] * count,
+        out_specs=[pl.BlockSpec((k_count, 1, 2, width), lambda j: (0, j, 0, 0))] * count,
+        out_shape=[jax.ShapeDtypeStruct((k_count, per_pair, 2, width), BF16)] * count,
         compiler_params=pltpu.CompilerParams(vmem_limit_bytes=16 << 20),
         name="to_cells",
-    )(k_matrix, rows)
+    )(k_matrix, *blocks)
 
 
 def place(blocks, start, total, out):
@@ -219,7 +234,7 @@
 
 def chunks_of(pairs):
     tiles = pairs // LANES
-    sizes = [1, 3, 3]
+    sizes = [3, 4]
     sizes = sizes + [tiles - sum(sizes)] if tiles > sum(sizes) else [tiles]
     starts = np.concatenate([[0], np.cumsum(sizes)[:-1]])
     return [(int(a) * LANES, int(b) * LANES) for a, b in zip(starts, sizes)]
@@ -227,64 +242,44 @@
 
 def after(array, *others):
     return lax.optimization_barrier((array, *others))[0]
-
-
-def order_of(count):
-    order = [("S", 0), ("S", 1), ("C", 0), ("M", 0), ("C", 1), ("X", 0), ("S", 2), ("K", 0), ("C", 2), ("X", 1)]
-    for at in range(1, count):
-        order += [("S", at + 2), ("C", at + 2), ("X", at + 1), ("P", at - 1), ("K", at)]
-    return order + [("P", count - 1)]
 
 
 def pipelined(kown, qown, g, k_points, q_points, re_cells, rp_cells, rp_degen, fine_q):
     per_pair = fine_q.shape[1] // (qown * kown)
     chunks = chunks_of(g.shape[3])
     count = len(chunks)
-    kept, near, sent, far, summed, rows, cells, done = {}, {}, {}, {}, {}, {}, {}, {-1: None}
     weights = fine_weights(kown, qown, True, fine_q, rp_cells, rp_degen, q_points)
-    last = weights
-    k_matrix = None
-
-    def over_q(at):
-        nonlocal last
-        start, width = chunks[at]
-        kept[at], send = interpolate(after(weights, last), g, start, width, kown, per_pair)
-        near[at] = swap(send, "qown", qown, 1)
-        last = kept[at]
-
-    def add_core(at):
-        nonlocal last
-        sent[at] = add("add_core", 1, kept[at], after(near[at], last))
-        gates = [far[at - 1]] if at == 1 and True else []
+    k_matrix = k_phases(kown, True, re_cells, k_points)
+    kept, sent, far, summed, cells, done = {}, {}, {}, {}, {}, {-1: None}
+
+    def given(results, at):
+        return [results[at]] if at in results else []
+
+    def cross(blocks):
+        return [block if by == 0 else swap(block, "kown", kown, by) for by, block in enumerate(blocks)]
+
+    def finish(at):
+        done[at] = place(cross(cells[at]), chunks[at][0], g.shape[3], done[at - 1])
+
+    for at, (start, width) in enumerate(chunks):
+        gate = after(weights, *given(kept, at - 1), *given(sent, at - 2), *given(summed, at - 2))
+        keep, core_keep, x_keep, both = interpolate(gate, g, start, width, qown, kown, per_pair)
+        kept[at] = keep
+        sent[at] = add_two(x_keep, swap(both, "qown", qown, 1))
+        near = swap(core_keep, "qown", qown, 1)
+        gates = given(far, at - 1) if 2 == 0 else (given(summed, at - 1) if 2 == 1 or at == 1 else given(summed, at - 2))
         far[at] = swap(after(sent[at], *gates), "qown", qown, 2)
-        last = sent[at]
-
-    def add_x(at):
-        nonlocal last
-        summed[at] = add("add_x", 0, kept[at], near[at], after(far[at], last))
-        rows[at] = lax.all_to_all(summed[at], "kown", split_axis=0, concat_axis=0, tiled=True)
-        last = summed[at]
-
-    def over_k(at):
-        nonlocal last
-        cells[at] = to_cells(k_matrix, after(rows[at], last))
-        last = cells[at][0]
-
-    def finish(at):
-        nonlocal last
-        blocks = [block if by == 0 else swap(block, "kown", kown, by) for by, block in enumerate(cells[at])]
-        blocks[-1] = after(blocks[-1], last)
-        done[at] = place(blocks, chunks[at][0], g.shape[3], done[at - 1])
-        if at + 1 < count:
-            last, done[at] = lax.optimization_barrier((last, done[at]))
-
-    stages = {"S": over_q, "C": add_core, "X": add_x, "K": over_k, "P": finish}
-    for stage, at in order_of(count):
-        if stage == "M":
-            k_matrix = k_phases(kown, True, after(re_cells, last), k_points)
-            last = k_matrix
-        elif at < count:
-            stages[stage](at)
+        blocks = add_split(keep, near, far[at])
+        summed[at] = blocks[0]
+        blocks = [after(block, *[other[0] for other in given(cells, at - 99)]) for block in blocks]
+        rows = cross(blocks)
+        if at >= 2:
+            finish(at - 2)
+            rows[0], done[at - 2] = lax.optimization_barrier((rows[0], done[at - 2]))
+        cells[at] = to_cells(k_matrix, rows)
+    for at in range(count):
+        if at not in done:
+            finish(at)
     return done[count - 1]
 
 

time: 362 us -> 335 us (0.925)
  waiting for transfers between devices: 138 us -> 173 us
  Pallas kernels: 90.9 us -> 66.5 us
  blocking collectives: 20 us -> 0 us
  local copies, waits for them, and re-layouts: 19.8 us -> 2.76 us
    ppermute x36 -> x51, waiting for transfers between devices: 138 us -> 173 us  [swap(): return lax.ppermute(array, axis, [(i, i ^ bit) for i in range(size)])]
    all_to_all x1 -> x0, blocking collectives: 20 us -> none  [add_x(): lax.all_to_all(summed[at], 'kown', split_axis=0, concat_axis=0, tiled=True)]
    ppermute x36 -> x51, starting transfers between devices: 72.8 us -> 91.1 us  [swap(): return lax.ppermute(array, axis, [(i, i ^ bit) for i in range(size)])]
    all_to_all x3 -> x0, starting transfers between devices: 18.3 us -> none  [add_x(): lax.all_to_all(summed[at], 'kown', split_axis=0, concat_axis=0, tiled=True)]
    unnamed x84 -> x12, local copies, waits for them, and re-layouts: 19.8 us -> 2.76 us
    pallas_call x4 -> x3, Pallas kernels: 37.6 us -> 30.6 us  [interpolate(): pl.pallas_call(kernel, grid=(k_count // step,), in_specs=[pl.BlockSpec(we...]
    pallas_call x4 -> x3, Pallas kernels: 15.8 us -> 9.12 us  [to_cells(): pl.pallas_call(kernel, grid=(per_pair,), in_specs=[pl.BlockSpec(k_matrix....]
    pallas_call x8 -> x6, Pallas kernels: 20.4 us -> 14.2 us  [the longest x3 8 us: add_split(): pl.pallas_call(kernel, grid=(k_count // step,), in_specs=[spec] * 3, out_...]
  transfers between devices with their start and end apart: 39 -> 51, of which waited for: 15 -> 27; matrix products, arithmetic and copies ran while one was open for 0% -> 0% of each run, Pallas kernels for 13% -> 16%
where the time goes in v2:
time: 335 us; the launch traced here: 334 us
  waiting for transfers between devices  173 us (52%)
  starting transfers between devices  91.1 us (27%)
  Pallas kernels  66.5 us (20%)
    ppermute x51, waiting for transfers between devices, swap(): return lax.ppermute(array, axis, [(i, i ^ bit) for i in range(size)])  173 us
    ppermute x51, starting transfers between devices, swap(): return lax.ppermute(array, axis, [(i, i ^ bit) for i in range(size)])  91.1 us
    pallas_call x3, Pallas kernels, interpolate(): pl.pallas_call(kernel, grid=(k_count // step,), in_specs=[pl.BlockSpec(we...  30.6 us
    pallas_call x3, Pallas kernels, to_cells(): pl.pallas_call(kernel, grid=(per_pair,), in_specs=[pl.BlockSpec(k_matrix....  9.12 us
    pallas_call x3, Pallas kernels, add_split(): pl.pallas_call(kernel, grid=(k_count // step,), in_specs=[spec] * 3, out_...  8 us
  transfers between devices with their start and end apart: 51, of which 27 were waited for; matrix products, arithmetic and copies ran while one was open for 0% of the time, Pallas kernels for 16%

profile of v2, /device:TPU:8, one launch (start us, length us, event | category | flops | bytes accessed | tf_op | source)
XLA Modules:
  0.0 334.0 jit_solution(16266070535161315324)
XLA Ops:
  4.4 10.0 %interpolate.3 = (bf16[8,2,64,2,384]{4,3,2,1,0:T(2,128)(2,1)S(1)}, bf16[8,2,64,2,384]{4,3,2,1,0:T(2,128)(2,1)S(1)}, bf16[8,2,64,2,384]{4,3,2,1,0:T(2,128)(2,1)S(1)}, bf16[8,2,64,2,384]{4,3,2,1,0:T(2,128)(2,1)S(1)}) custom-call(bf16[128,256]{1,0:T(8,128)(2,1)S(1)} %fine_weights.1.w_ref, bf16[64,128,2,1280]{3,2,1,0:T(2,128)(2,1)} %g_ref.5), custom_call_target="tpu_custom_call" | custom-call | tf_op jit(solution)/shard_map/interpolate/pallas_call | solution.py:118
  14.5 10.5 %interpolate.4 = (bf16[8,2,64,2,512]{4,3,2,1,0:T(2,128)(2,1)S(1)}, bf16[8,2,64,2,512]{4,3,2,1,0:T(2,128)(2,1)S(1)}, bf16[8,2,64,2,512]{4,3,2,1,0:T(2,128)(2,1)S(1)}, bf16[8,2,64,2,512]{4,3,2,1,0:T(2,128)(2,1)S(1)}) custom-call(bf16[128,256]{1,0:T(8,128)(2,1)S(1)} %fine_weights.1.w_ref, bf16[64,128,2,1280]{3,2,1,0:T(2,128)(2,1)} %g_ref.5), custom_call_target="tpu_custom_call" | custom-call | tf_op jit(solution)/shard_map/interpolate/pallas_call | solution.py:118
  31.6 33.2 %collective-permute-done.2.c_ref = bf16[8,2,64,2,384]{4,3,2,1,0:T(2,128)(2,1)S(1)} collective-permute-done((bf16[8,2,64,2,384]{4,3,2,1,0:T(2,128)(2,1)S(1)}, bf16[8,2,64,2,384]{4,3,2,1,0:T(2,128)(2,1)S(1)}, u32[]{:S(2)}, u32[]{:S(2)}) %collective-permute-start.2) | collective-permute-done | bytes 1572896 | tf_op jit(solution)/shard_map/ppermute | solution.py:232
  69.3 10.0 %interpolate.5 = (bf16[8,2,64,2,384]{4,3,2,1,0:T(2,128)(2,1)S(1)}, bf16[8,2,64,2,384]{4,3,2,1,0:T(2,128)(2,1)S(1)}, bf16[8,2,64,2,384]{4,3,2,1,0:T(2,128)(2,1)S(1)}, bf16[8,2,64,2,384]{4,3,2,1,0:T(2,128)(2,1)S(1)}) custom-call(bf16[128,256]{1,0:T(8,128)(2,1)S(1)} %fine_weights.1.w_ref, bf16[64,128,2,1280]{3,2,1,0:T(2,128)(2,1)} %g_ref.5), custom_call_target="tpu_custom_call" | custom-call | tf_op jit(solution)/shard_map/interpolate/pallas_call | solution.py:118
  87.3 8.9 %collective-permute-done.10.refs_5_ = bf16[2,64,2,384]{3,2,1,0:T(2,128)(2,1)S(1)} collective-permute-done((bf16[2,64,2,384]{3,2,1,0:T(2,128)(2,1)S(1)}, bf16[2,64,2,384]{3,2,1,0:T(2,128)(2,1)S(1)}, u32[]{:S(2)}, u32[]{:S(2)}) %collective-permute-start.10) | collective-permute-done | bytes 196640 | tf_op jit(solution)/shard_map/ppermute | solution.py:232
  96.2 4.5 %collective-permute-done.11.refs_6_ = bf16[2,64,2,384]{3,2,1,0:T(2,128)(2,1)S(1)} collective-permute-done((bf16[2,64,2,384]{3,2,1,0:T(2,128)(2,1)S(1)}, bf16[2,64,2,384]{3,2,1,0:T(2,128)(2,1)S(1)}, u32[]{:S(2)}, u32[]{:S(2)}) %collective-permute-start.11) | collective-permute-done | bytes 196640 | tf_op jit(solution)/shard_map/ppermute | solution.py:232
  101.2 7.6 %collective-permute-done.12.refs_7_ = bf16[2,64,2,384]{3,2,1,0:T(2,128)(2,1)S(1)} collective-permute-done((bf16[2,64,2,384]{3,2,1,0:T(2,128)(2,1)S(1)}, bf16[2,64,2,384]{3,2,1,0:T(2,128)(2,1)S(1)}, u32[]{:S(2)}, u32[]{:S(2)}) %collective-permute-start.12) | collective-permute-done | bytes 196640 | tf_op jit(solution)/shard_map/ppermute | solution.py:232
  111.9 4.5 %collective-permute-done.36.c_ref = bf16[8,2,64,2,512]{4,3,2,1,0:T(2,128)(2,1)S(1)} collective-permute-done((bf16[8,2,64,2,512]{4,3,2,1,0:T(2,128)(2,1)S(1)}, bf16[8,2,64,2,512]{4,3,2,1,0:T(2,128)(2,1)S(1)}, u32[]{:S(2)}, u32[]{:S(2)}) %collective-permute-start.36) | collective-permute-done | bytes 2097184 | tf_op jit(solution)/shard_map/ppermute | solution.py:232
  122.7 5.4 %k_phases.1.m_ref = bf16[1024,1024]{1,0:T(8,128)(2,1)S(1)} custom-call(s32[3,512]{1,0:T(4,128)S(1)} %copy-done, s32[3,512]{1,0:T(4,128)S(1)} %copy-done.1), custom_call_target="tpu_custom_call" | custom-call | tf_op jit(solution)/shard_map/k_phases/pallas_call | solution.py:92
  132.3 5.0 %collective-permute-done.13.refs_1_ = bf16[64,2,2,384]{3,2,1,0:T(2,128)(2,1)S(1)} collective-permute-done((bf16[64,2,2,384]{3,2,1,0:T(2,128)(2,1)S(1)}, bf16[64,2,2,384]{3,2,1,0:T(2,128)(2,1)S(1)}, u32[]{:S(2)}, u32[]{:S(2)}) %collective-permute-start.13) | collective-permute-done | bytes 196640 | tf_op jit(solution)/shard_map/ppermute | solution.py:232
  138.0 5.0 %collective-permute-done.38.refs_2_ = bf16[2,64,2,512]{3,2,1,0:T(2,128)(2,1)S(1)} collective-permute-done((bf16[2,64,2,512]{3,2,1,0:T(2,128)(2,1)S(1)}, bf16[2,64,2,512]{3,2,1,0:T(2,128)(2,1)S(1)}, u32[]{:S(2)}, u32[]{:S(2)}) %collective-permute-start.38) | collective-permute-done | bytes 262176 | tf_op jit(solution)/shard_map/ppermute | solution.py:232
  143.0 6.5 %collective-permute-start.41 = (bf16[2,64,2,512]{3,2,1,0:T(2,128)(2,1)S(1)}, bf16[2,64,2,512]{3,2,1,0:T(2,128)(2,1)S(1)}, u32[]{:S(2)}, u32[]{:S(2)}) collective-permute-start(bf16[2,64,2,512]{3,2,1,0:T(2,128)(2,1)S(1)} %get-tuple-element.125), channel_id=1, source_target_pairs={{0,20},{4,16},{8,28},{12,24},{16,4},{20,0},{24,12},{28,8},{1,21},{... | collective-permute-start | bytes 786440 | tf_op jit(solution)/shard_map/ppermute | solution.py:232
  151.4 15.6 %collective-permute-start.43 = (bf16[2,64,2,512]{3,2,1,0:T(2,128)(2,1)S(1)}, bf16[2,64,2,512]{3,2,1,0:T(2,128)(2,1)S(1)}, u32[]{:S(2)}, u32[]{:S(2)}) collective-permute-start(bf16[2,64,2,512]{3,2,1,0:T(2,128)(2,1)S(1)} %get-tuple-element.127), channel_id=1, source_target_pairs={{0,28},{4,24},{8,20},{12,16},{16,12},{20,8},{24,4},{28,0},{1,29},{... | collective-permute-start | bytes 786440 | tf_op jit(solution)/shard_map/ppermute | solution.py:232
  168.1 7.6 %collective-permute-start.14 = (bf16[64,2,2,384]{3,2,1,0:T(2,128)(2,1)S(1)}, bf16[64,2,2,384]{3,2,1,0:T(2,128)(2,1)S(1)}, u32[]{:S(2)}, u32[]{:S(2)}) collective-permute-start(bf16[64,2,2,384]{3,2,1,0:T(2,128)(2,1)S(1)} %get-tuple-element.94), channel_id=1, source_target_pairs={{0,8},{4,12},{8,0},{12,4},{16,24},{20,28},{24,16},{28,20},{1,9},{5... | collective-permute-start | bytes 589832 | tf_op jit(solution)/shard_map/ppermute | solution.py:232
  180.1 6.3 %collective-permute-done.43.refs_7_ = bf16[2,64,2,512]{3,2,1,0:T(2,128)(2,1)S(1)} collective-permute-done((bf16[2,64,2,512]{3,2,1,0:T(2,128)(2,1)S(1)}, bf16[2,64,2,512]{3,2,1,0:T(2,128)(2,1)S(1)}, u32[]{:S(2)}, u32[]{:S(2)}) %collective-permute-start.43) | collective-permute-done | bytes 262176 | tf_op jit(solution)/shard_map/ppermute | solution.py:232
  194.5 5.7 %collective-permute-done.16.refs_4_ = bf16[64,2,2,384]{3,2,1,0:T(2,128)(2,1)S(1)} collective-permute-done((bf16[64,2,2,384]{3,2,1,0:T(2,128)(2,1)S(1)}, bf16[64,2,2,384]{3,2,1,0:T(2,128)(2,1)S(1)}, u32[]{:S(2)}, u32[]{:S(2)}) %collective-permute-start.16) | collective-permute-done | bytes 196640 | tf_op jit(solution)/shard_map/ppermute | solution.py:232
  202.7 4.5 %collective-permute-start.45 = (bf16[64,2,2,512]{3,2,1,0:T(2,128)(2,1)S(1)}, bf16[64,2,2,512]{3,2,1,0:T(2,128)(2,1)S(1)}, u32[]{:S(2)}, u32[]{:S(2)}) collective-permute-start(bf16[64,2,2,512]{3,2,1,0:T(2,128)(2,1)S(1)} %get-tuple-element.130), channel_id=1, source_target_pairs={{0,8},{4,12},{8,0},{12,4},{16,24},{20,28},{24,16},{28,20},{1,9},{5... | collective-permute-start | bytes 786440 | tf_op jit(solution)/shard_map/ppermute | solution.py:232
  230.4 10.1 %collective-permute-done.23.refs_4_ = bf16[2,64,2,384]{3,2,1,0:T(2,128)(2,1)S(1)} collective-permute-done((bf16[2,64,2,384]{3,2,1,0:T(2,128)(2,1)S(1)}, bf16[2,64,2,384]{3,2,1,0:T(2,128)(2,1)S(1)}, u32[]{:S(2)}, u32[]{:S(2)}) %collective-permute-start.23) | collective-permute-done | bytes 196640 | tf_op jit(solution)/shard_map/ppermute | solution.py:232
  244.4 15.4 %collective-permute-done.24.refs_5_ = bf16[2,64,2,384]{3,2,1,0:T(2,128)(2,1)S(1)} collective-permute-done((bf16[2,64,2,384]{3,2,1,0:T(2,128)(2,1)S(1)}, bf16[2,64,2,384]{3,2,1,0:T(2,128)(2,1)S(1)}, u32[]{:S(2)}, u32[]{:S(2)}) %collective-permute-start.24) | collective-permute-done | bytes 196640 | tf_op jit(solution)/shard_map/ppermute | solution.py:232
  264.2 10.1 %collective-permute-done.25.refs_6_ = bf16[2,64,2,384]{3,2,1,0:T(2,128)(2,1)S(1)} collective-permute-done((bf16[2,64,2,384]{3,2,1,0:T(2,128)(2,1)S(1)}, bf16[2,64,2,384]{3,2,1,0:T(2,128)(2,1)S(1)}, u32[]{:S(2)}, u32[]{:S(2)}) %collective-permute-start.25) | collective-permute-done | bytes 196640 | tf_op jit(solution)/shard_map/ppermute | solution.py:232
  292.1 5.4 %collective-permute-done.49.refs_6_ = bf16[64,2,2,512]{3,2,1,0:T(2,128)(2,1)S(1)} collective-permute-done((bf16[64,2,2,512]{3,2,1,0:T(2,128)(2,1)S(1)}, bf16[64,2,2,512]{3,2,1,0:T(2,128)(2,1)S(1)}, u32[]{:S(2)}, u32[]{:S(2)}) %collective-permute-start.49) | collective-permute-done | bytes 262176 | tf_op jit(solution)/shard_map/ppermute | solution.py:232
  297.5 14.4 %collective-permute-done.50.refs_7_ = bf16[64,2,2,512]{3,2,1,0:T(2,128)(2,1)S(1)} collective-permute-done((bf16[64,2,2,512]{3,2,1,0:T(2,128)(2,1)S(1)}, bf16[64,2,2,512]{3,2,1,0:T(2,128)(2,1)S(1)}, u32[]{:S(2)}, u32[]{:S(2)}) %collective-permute-start.50) | collective-permute-done | bytes 262176 | tf_op jit(solution)/shard_map/ppermute | solution.py:232
  316.4 8.2 %collective-permute-done.31.refs_5_ = bf16[64,2,2,384]{3,2,1,0:T(2,128)(2,1)S(1)} collective-permute-done((bf16[64,2,2,384]{3,2,1,0:T(2,128)(2,1)S(1)}, bf16[64,2,2,384]{3,2,1,0:T(2,128)(2,1)S(1)}, u32[]{:S(2)}, u32[]{:S(2)}) %collective-permute-start.31) | collective-permute-done | bytes 196640 | tf_op jit(solution)/shard_map/ppermute | solution.py:232
  324.6 4.5 %collective-permute-done.32.refs_6_ = bf16[64,2,2,384]{3,2,1,0:T(2,128)(2,1)S(1)} collective-permute-done((bf16[64,2,2,384]{3,2,1,0:T(2,128)(2,1)S(1)}, bf16[64,2,2,384]{3,2,1,0:T(2,128)(2,1)S(1)}, u32[]{:S(2)}, u32[]{:S(2)}) %collective-permute-start.32) | collective-permute-done | bytes 196640 | tf_op jit(solution)/shard_map/ppermute | solution.py:232
  (107 shorter events, 114.9 us)
Async XLA Ops:
  28.0 36.8 %collective-permute-start.2 = (bf16[8,2,64,2,384]{4,3,2,1,0:T(2,128)(2,1)S(1)}, bf16[8,2,64,2,384]{4,3,2,1,0:T(2,128)(2,1)S(1)}, u32[]{:S(2)}, u32[]{:S(2)}) collective-permute-start(bf16[8,2,64,2,384]{4,3,2,1,0:T(2,128)(2,1)S(1)} %add_two.3), channel_id=1, source_target_pairs={{0,2},{1,3},{2,0},{3,1},{4,6},{5,7},{6,4},{7,5},{8,10},{9,11},{10,... | collective-permute-start | bytes 4718600 | tf_op jit(solution)/shard_map/ppermute | solution.py:232
  29.6 57.2 %collective-permute-start.34 = (bf16[8,2,64,2,512]{4,3,2,1,0:T(2,128)(2,1)S(1)}, bf16[8,2,64,2,512]{4,3,2,1,0:T(2,128)(2,1)S(1)}, u32[]{:S(2)}, u32[]{:S(2)}) collective-permute-start(bf16[8,2,64,2,512]{4,3,2,1,0:T(2,128)(2,1)S(1)} %get-tuple-element.116), channel_id=1, source_target_pairs={{0,1},{1,0},{2,3},{3,2},{4,5},{5,4},{6,7},{7,6},{8,9},{9,8},{10,11... | collective-permute-start | bytes 6291464 | tf_op jit(solution)/shard_map/ppermute | solution.py:232
  67.8 48.6 %collective-permute-start.36 = (bf16[8,2,64,2,512]{4,3,2,1,0:T(2,128)(2,1)S(1)}, bf16[8,2,64,2,512]{4,3,2,1,0:T(2,128)(2,1)S(1)}, u32[]{:S(2)}, u32[]{:S(2)}) collective-permute-start(bf16[8,2,64,2,512]{4,3,2,1,0:T(2,128)(2,1)S(1)} %add_two.5), channel_id=1, source_target_pairs={{0,2},{1,3},{2,0},{3,1},{4,6},{5,7},{6,4},{7,5},{8,10},{9,11},{10,... | collective-permute-start | bytes 6291464 | tf_op jit(solution)/shard_map/ppermute | solution.py:232
  83.0 118.8 %collective-permute-start.3 = (bf16[8,2,64,2,384]{4,3,2,1,0:T(2,128)(2,1)S(1)}, bf16[8,2,64,2,384]{4,3,2,1,0:T(2,128)(2,1)S(1)}, u32[]{:S(2)}, u32[]{:S(2)}) collective-permute-start(bf16[8,2,64,2,384]{4,3,2,1,0:T(2,128)(2,1)S(1)} %get-tuple-element.80), channel_id=1, source_target_pairs={{0,1},{1,0},{2,3},{3,2},{4,5},{5,4},{6,7},{7,6},{8,9},{9,8},{10,11... | collective-permute-start | bytes 4718600 | tf_op jit(solution)/shard_map/ppermute | solution.py:232
  86.7 116.0 %collective-permute-start.5 = (bf16[8,2,64,2,384]{4,3,2,1,0:T(2,128)(2,1)S(1)}, bf16[8,2,64,2,384]{4,3,2,1,0:T(2,128)(2,1)S(1)}, u32[]{:S(2)}, u32[]{:S(2)}) collective-permute-start(bf16[8,2,64,2,384]{4,3,2,1,0:T(2,128)(2,1)S(1)} %add_two.4), channel_id=1, source_target_pairs={{0,2},{1,3},{2,0},{3,1},{4,6},{5,7},{6,4},{7,5},{8,10},{9,11},{10,... | collective-permute-start | bytes 4718600 | tf_op jit(solution)/shard_map/ppermute | solution.py:232
  143.0 25.1 %collective-permute-start.41 = (bf16[2,64,2,512]{3,2,1,0:T(2,128)(2,1)S(1)}, bf16[2,64,2,512]{3,2,1,0:T(2,128)(2,1)S(1)}, u32[]{:S(2)}, u32[]{:S(2)}) collective-permute-start(bf16[2,64,2,512]{3,2,1,0:T(2,128)(2,1)S(1)} %get-tuple-element.125), channel_id=1, source_target_pairs={{0,20},{4,16},{8,28},{12,24},{16,4},{20,0},{24,12},{28,8},{1,21},{... | collective-permute-start | bytes 786440 | tf_op jit(solution)/shard_map/ppermute | solution.py:232
  149.5 30.6 %collective-permute-start.42 = (bf16[2,64,2,512]{3,2,1,0:T(2,128)(2,1)S(1)}, bf16[2,64,2,512]{3,2,1,0:T(2,128)(2,1)S(1)}, u32[]{:S(2)}, u32[]{:S(2)}) collective-permute-start(bf16[2,64,2,512]{3,2,1,0:T(2,128)(2,1)S(1)} %get-tuple-element.126), channel_id=1, source_target_pairs={{0,24},{4,28},{8,16},{12,20},{16,8},{20,12},{24,0},{28,4},{1,25},{... | collective-permute-start | bytes 786440 | tf_op jit(solution)/shard_map/ppermute | solution.py:232
  151.4 34.9 %collective-permute-start.43 = (bf16[2,64,2,512]{3,2,1,0:T(2,128)(2,1)S(1)}, bf16[2,64,2,512]{3,2,1,0:T(2,128)(2,1)S(1)}, u32[]{:S(2)}, u32[]{:S(2)}) collective-permute-start(bf16[2,64,2,512]{3,2,1,0:T(2,128)(2,1)S(1)} %get-tuple-element.127), channel_id=1, source_target_pairs={{0,28},{4,24},{8,20},{12,16},{16,12},{20,8},{24,4},{28,0},{1,29},{... | collective-permute-start | bytes 786440 | tf_op jit(solution)/shard_map/ppermute | solution.py:232
  168.1 21.3 %collective-permute-start.14 = (bf16[64,2,2,384]{3,2,1,0:T(2,128)(2,1)S(1)}, bf16[64,2,2,384]{3,2,1,0:T(2,128)(2,1)S(1)}, u32[]{:S(2)}, u32[]{:S(2)}) collective-permute-start(bf16[64,2,2,384]{3,2,1,0:T(2,128)(2,1)S(1)} %get-tuple-element.94), channel_id=1, source_target_pairs={{0,8},{4,12},{8,0},{12,4},{16,24},{20,28},{24,16},{28,20},{1,9},{5... | collective-permute-start | bytes 589832 | tf_op jit(solution)/shard_map/ppermute | solution.py:232
  189.4 27.6 %collective-permute-start.44 = (bf16[64,2,2,512]{3,2,1,0:T(2,128)(2,1)S(1)}, bf16[64,2,2,512]{3,2,1,0:T(2,128)(2,1)S(1)}, u32[]{:S(2)}, u32[]{:S(2)}) collective-permute-start(bf16[64,2,2,512]{3,2,1,0:T(2,128)(2,1)S(1)} %get-tuple-element.129), channel_id=1, source_target_pairs={{0,4},{4,0},{8,12},{12,8},{16,20},{20,16},{24,28},{28,24},{1,5},{5... | collective-permute-start | bytes 786440 | tf_op jit(solution)/shard_map/ppermute | solution.py:232
  216.9 23.6 %collective-permute-start.23 = (bf16[2,64,2,384]{3,2,1,0:T(2,128)(2,1)S(1)}, bf16[2,64,2,384]{3,2,1,0:T(2,128)(2,1)S(1)}, u32[]{:S(2)}, u32[]{:S(2)}) collective-permute-start(bf16[2,64,2,384]{3,2,1,0:T(2,128)(2,1)S(1)} %get-tuple-element.104), channel_id=1, source_target_pairs={{0,16},{4,20},{8,24},{12,28},{16,0},{20,4},{24,8},{28,12},{1,17},{... | collective-permute-start | bytes 589832 | tf_op jit(solution)/shard_map/ppermute | solution.py:232
  219.8 40.0 %collective-permute-start.24 = (bf16[2,64,2,384]{3,2,1,0:T(2,128)(2,1)S(1)}, bf16[2,64,2,384]{3,2,1,0:T(2,128)(2,1)S(1)}, u32[]{:S(2)}, u32[]{:S(2)}) collective-permute-start(bf16[2,64,2,384]{3,2,1,0:T(2,128)(2,1)S(1)} %get-tuple-element.105), channel_id=1, source_target_pairs={{0,20},{4,16},{8,28},{12,24},{16,4},{20,0},{24,12},{28,8},{1,21},{... | collective-permute-start | bytes 589832 | tf_op jit(solution)/shard_map/ppermute | solution.py:232
  220.6 53.7 %collective-permute-start.25 = (bf16[2,64,2,384]{3,2,1,0:T(2,128)(2,1)S(1)}, bf16[2,64,2,384]{3,2,1,0:T(2,128)(2,1)S(1)}, u32[]{:S(2)}, u32[]{:S(2)}) collective-permute-start(bf16[2,64,2,384]{3,2,1,0:T(2,128)(2,1)S(1)} %get-tuple-element.106), channel_id=1, source_target_pairs={{0,24},{4,28},{8,16},{12,20},{16,8},{20,12},{24,0},{28,4},{1,25},{... | collective-permute-start | bytes 589832 | tf_op jit(solution)/shard_map/ppermute | solution.py:232
  224.4 54.5 %collective-permute-start.26 = (bf16[2,64,2,384]{3,2,1,0:T(2,128)(2,1)S(1)}, bf16[2,64,2,384]{3,2,1,0:T(2,128)(2,1)S(1)}, u32[]{:S(2)}, u32[]{:S(2)}) collective-permute-start(bf16[2,64,2,384]{3,2,1,0:T(2,128)(2,1)S(1)} %get-tuple-element.107), channel_id=1, source_target_pairs={{0,28},{4,24},{8,20},{12,16},{16,12},{20,8},{24,4},{28,0},{1,29},{... | collective-permute-start | bytes 589832 | tf_op jit(solution)/shard_map/ppermute | solution.py:232
  227.0 58.1 %collective-permute-start.46 = (bf16[64,2,2,512]{3,2,1,0:T(2,128)(2,1)S(1)}, bf16[64,2,2,512]{3,2,1,0:T(2,128)(2,1)S(1)}, u32[]{:S(2)}, u32[]{:S(2)}) collective-permute-start(bf16[64,2,2,512]{3,2,1,0:T(2,128)(2,1)S(1)} %get-tuple-element.131), channel_id=1, source_target_pairs={{0,12},{4,8},{8,4},{12,0},{16,28},{20,24},{24,20},{28,16},{1,13},{... | collective-permute-start | bytes 786440 | tf_op jit(solution)/shard_map/ppermute | solution.py:232
  240.5 46.0 %collective-permute-start.47 = (bf16[64,2,2,512]{3,2,1,0:T(2,128)(2,1)S(1)}, bf16[64,2,2,512]{3,2,1,0:T(2,128)(2,1)S(1)}, u32[]{:S(2)}, u32[]{:S(2)}) collective-permute-start(bf16[64,2,2,512]{3,2,1,0:T(2,128)(2,1)S(1)} %get-tuple-element.132), channel_id=1, source_target_pairs={{0,16},{4,20},{8,24},{12,28},{16,0},{20,4},{24,8},{28,12},{1,17},{... | collective-permute-start | bytes 786440 | tf_op jit(solution)/shard_map/ppermute | solution.py:232
  259.8 28.3 %collective-permute-start.48 = (bf16[64,2,2,512]{3,2,1,0:T(2,128)(2,1)S(1)}, bf16[64,2,2,512]{3,2,1,0:T(2,128)(2,1)S(1)}, u32[]{:S(2)}, u32[]{:S(2)}) collective-permute-start(bf16[64,2,2,512]{3,2,1,0:T(2,128)(2,1)S(1)} %get-tuple-element.133), channel_id=1, source_target_pairs={{0,20},{4,16},{8,28},{12,24},{16,4},{20,0},{24,12},{28,8},{1,21},{... | collective-permute-start | bytes 786440 | tf_op jit(solution)/shard_map/ppermute | solution.py:232
  274.3 23.2 %collective-permute-start.49 = (bf16[64,2,2,512]{3,2,1,0:T(2,128)(2,1)S(1)}, bf16[64,2,2,512]{3,2,1,0:T(2,128)(2,1)S(1)}, u32[]{:S(2)}, u32[]{:S(2)}) collective-permute-start(bf16[64,2,2,512]{3,2,1,0:T(2,128)(2,1)S(1)} %get-tuple-element.134), channel_id=1, source_target_pairs={{0,24},{4,28},{8,16},{12,20},{16,8},{20,12},{24,0},{28,4},{1,25},{... | collective-permute-start | bytes 786440 | tf_op jit(solution)/shard_map/ppermute | solution.py:232
  278.9 33.0 %collective-permute-start.50 = (bf16[64,2,2,512]{3,2,1,0:T(2,128)(2,1)S(1)}, bf16[64,2,2,512]{3,2,1,0:T(2,128)(2,1)S(1)}, u32[]{:S(2)}, u32[]{:S(2)}) collective-permute-start(bf16[64,2,2,512]{3,2,1,0:T(2,128)(2,1)S(1)} %get-tuple-element.135), channel_id=1, source_target_pairs={{0,28},{4,24},{8,20},{12,16},{16,12},{20,8},{24,4},{28,0},{1,29},{... | collective-permute-start | bytes 786440 | tf_op jit(solution)/shard_map/ppermute | solution.py:232
  285.1 26.8 %collective-permute-start.27 = (bf16[64,2,2,384]{3,2,1,0:T(2,128)(2,1)S(1)}, bf16[64,2,2,384]{3,2,1,0:T(2,128)(2,1)S(1)}, u32[]{:S(2)}, u32[]{:S(2)}) collective-permute-start(bf16[64,2,2,384]{3,2,1,0:T(2,128)(2,1)S(1)} %get-tuple-element.109), channel_id=1, source_target_pairs={{0,4},{4,0},{8,12},{12,8},{16,20},{20,16},{24,28},{28,24},{1,5},{5... | collective-permute-start | bytes 589832 | tf_op jit(solution)/shard_map/ppermute | solution.py:232
  286.5 26.7 %collective-permute-start.28 = (bf16[64,2,2,384]{3,2,1,0:T(2,128)(2,1)S(1)}, bf16[64,2,2,384]{3,2,1,0:T(2,128)(2,1)S(1)}, u32[]{:S(2)}, u32[]{:S(2)}) collective-permute-start(bf16[64,2,2,384]{3,2,1,0:T(2,128)(2,1)S(1)} %get-tuple-element.110), channel_id=1, source_target_pairs={{0,8},{4,12},{8,0},{12,4},{16,24},{20,28},{24,16},{28,20},{1,9},{5... | collective-permute-start | bytes 589832 | tf_op jit(solution)/shard_map/ppermute | solution.py:232
  288.1 28.3 %collective-permute-start.29 = (bf16[64,2,2,384]{3,2,1,0:T(2,128)(2,1)S(1)}, bf16[64,2,2,384]{3,2,1,0:T(2,128)(2,1)S(1)}, u32[]{:S(2)}, u32[]{:S(2)}) collective-permute-start(bf16[64,2,2,384]{3,2,1,0:T(2,128)(2,1)S(1)} %get-tuple-element.111), channel_id=1, source_target_pairs={{0,12},{4,8},{8,4},{12,0},{16,28},{20,24},{24,20},{28,16},{1,13},{... | collective-permute-start | bytes 589832 | tf_op jit(solution)/shard_map/ppermute | solution.py:232
  297.5 18.9 %collective-permute-start.30 = (bf16[64,2,2,384]{3,2,1,0:T(2,128)(2,1)S(1)}, bf16[64,2,2,384]{3,2,1,0:T(2,128)(2,1)S(1)}, u32[]{:S(2)}, u32[]{:S(2)}) collective-permute-start(bf16[64,2,2,384]{3,2,1,0:T(2,128)(2,1)S(1)} %get-tuple-element.112), channel_id=1, source_target_pairs={{0,16},{4,20},{8,24},{12,28},{16,0},{20,4},{24,8},{28,12},{1,17},{... | collective-permute-start | bytes 589832 | tf_op jit(solution)/shard_map/ppermute | solution.py:232
  313.2 19.0 %collective-permute-start.33 = (bf16[64,2,2,384]{3,2,1,0:T(2,128)(2,1)S(1)}, bf16[64,2,2,384]{3,2,1,0:T(2,128)(2,1)S(1)}, u32[]{:S(2)}, u32[]{:S(2)}) collective-permute-start(bf16[64,2,2,384]{3,2,1,0:T(2,128)(2,1)S(1)} %get-tuple-element.115), channel_id=1, source_target_pairs={{0,28},{4,24},{8,20},{12,16},{16,12},{20,8},{24,4},{28,0},{1,29},{... | collective-permute-start | bytes 589832 | tf_op jit(solution)/shard_map/ppermute | solution.py:232
  (33 other events, 365.1 us)

commit v3 on v2

--- a/solution.py
+++ b/solution.py
@@ -234,7 +234,7 @@
 
 def chunks_of(pairs):
     tiles = pairs // LANES
-    sizes = [3, 4]
+    sizes = [2, 4]
     sizes = sizes + [tiles - sum(sizes)] if tiles > sum(sizes) else [tiles]
     starts = np.concatenate([[0], np.cumsum(sizes)[:-1]])
     return [(int(a) * LANES, int(b) * LANES) for a, b in zip(starts, sizes)]
@@ -249,14 +249,15 @@
     chunks = chunks_of(g.shape[3])
     count = len(chunks)
     weights = fine_weights(kown, qown, True, fine_q, rp_cells, rp_degen, q_points)
-    k_matrix = k_phases(kown, True, re_cells, k_points)
-    kept, sent, far, summed, cells, done = {}, {}, {}, {}, {}, {-1: None}
+    k_matrix = None
+    kept, sent, far, summed, cells, moved, done = {}, {}, {}, {}, {}, {}, {-1: None}
 
     def given(results, at):
         return [results[at]] if at in results else []
 
     def cross(blocks):
-        return [block if by == 0 else swap(block, "kown", kown, by) for by, block in enumerate(blocks)]
+        moved = {by: swap(blocks[by], "kown", kown, by) for by in sorted(range(1, kown), key=lambda by: (by < kown // 2, by))}
+        return [blocks[0]] + [moved[by] for by in range(1, kown)]
 
     def finish(at):
         done[at] = place(cross(cells[at]), chunks[at][0], g.shape[3], done[at - 1])
@@ -266,13 +267,16 @@
         keep, core_keep, x_keep, both = interpolate(gate, g, start, width, qown, kown, per_pair)
         kept[at] = keep
         sent[at] = add_two(x_keep, swap(both, "qown", qown, 1))
+        if at == 0:
+            k_matrix = k_phases(kown, True, after(re_cells, sent[0]), k_points)
         near = swap(core_keep, "qown", qown, 1)
-        gates = given(far, at - 1) if 2 == 0 else (given(summed, at - 1) if 2 == 1 or at == 1 else given(summed, at - 2))
+        gates = given(far, at - 1) if 2 == 0 or (2 == 4 and at > 1) else (given(summed, at - 1) if 2 == 1 or at == 1 else given(summed, at - 2))
         far[at] = swap(after(sent[at], *gates), "qown", qown, 2)
         blocks = add_split(keep, near, far[at])
         summed[at] = blocks[0]
         blocks = [after(block, *[other[0] for other in given(cells, at - 99)]) for block in blocks]
         rows = cross(blocks)
+        moved[at] = list(rows)
         if at >= 2:
             finish(at - 2)
             rows[0], done[at - 2] = lax.optimization_barrier((rows[0], done[at - 2]))

time: 335 us -> 331 us (0.988)
  Pallas kernels: 66.5 us -> 59.9 us
  starting transfers between devices: 91.1 us -> 95.7 us
    ppermute x51, starting transfers between devices: 91.1 us -> 95.7 us  [swap(): return lax.ppermute(array, axis, [(i, i ^ bit) for i in range(size)])]
    ppermute x51, waiting for transfers between devices: 173 us -> 170 us  [swap(): return lax.ppermute(array, axis, [(i, i ^ bit) for i in range(size)])]
  transfers between devices with their start and end apart: 51 -> 51, of which waited for: 27 -> 31; matrix products, arithmetic and copies ran while one was open for 0% -> 0% of each run, Pallas kernels for 16% -> 15%
where the time goes in v3:
time: 331 us; the launch traced here: 329 us
  waiting for transfers between devices  170 us (51%)
  starting transfers between devices  95.7 us (29%)
  Pallas kernels  59.9 us (18%)
    ppermute x51, waiting for transfers between devices, swap(): return lax.ppermute(array, axis, [(i, i ^ bit) for i in range(size)])  170 us
    ppermute x51, starting transfers between devices, swap(): return lax.ppermute(array, axis, [(i, i ^ bit) for i in range(size)])  95.7 us
    pallas_call x3, Pallas kernels, interpolate(): pl.pallas_call(kernel, grid=(k_count // step,), in_specs=[pl.BlockSpec(we...  29.2 us
    pallas_call x3, Pallas kernels, to_cells(): pl.pallas_call(kernel, grid=(per_pair,), in_specs=[pl.BlockSpec(k_matrix....  8.03 us
  transfers between devices with their start and end apart: 51, of which 31 were waited for; matrix products, arithmetic and copies ran while one was open for 0% of the time, Pallas kernels for 15%

profile of v3, /device:TPU:8, one launch (start us, length us, event | category | flops | bytes accessed | tf_op | source)
XLA Modules:
  0.0 328.5 jit_solution(12948221424702822322)
XLA Ops:
  4.4 8.2 %interpolate.3 = (bf16[8,2,64,2,256]{4,3,2,1,0:T(2,128)(2,1)S(1)}, bf16[8,2,64,2,256]{4,3,2,1,0:T(2,128)(2,1)S(1)}, bf16[8,2,64,2,256]{4,3,2,1,0:T(2,128)(2,1)S(1)}, bf16[8,2,64,2,256]{4,3,2,1,0:T(2,128)(2,1)S(1)}) custom-call(bf16[128,256]{1,0:T(8,128)(2,1)S(1)} %fine_weights.1.w_ref, bf16[64,128,2,1280]{3,2,1,0:T(2,128)(2,1)} %g_ref.5), custom_call_target="tpu_custom_call" | custom-call | tf_op jit(solution)/shard_map/interpolate/pallas_call | solution.py:118
  18.0 10.5 %interpolate.4 = (bf16[8,2,64,2,512]{4,3,2,1,0:T(2,128)(2,1)S(1)}, bf16[8,2,64,2,512]{4,3,2,1,0:T(2,128)(2,1)S(1)}, bf16[8,2,64,2,512]{4,3,2,1,0:T(2,128)(2,1)S(1)}, bf16[8,2,64,2,512]{4,3,2,1,0:T(2,128)(2,1)S(1)}) custom-call(bf16[128,256]{1,0:T(8,128)(2,1)S(1)} %fine_weights.1.w_ref, bf16[64,128,2,1280]{3,2,1,0:T(2,128)(2,1)} %g_ref.5), custom_call_target="tpu_custom_call" | custom-call | tf_op jit(solution)/shard_map/interpolate/pallas_call | solution.py:118
  28.6 13.1 %collective-permute-done.2.c_ref = bf16[8,2,64,2,256]{4,3,2,1,0:T(2,128)(2,1)S(1)} collective-permute-done((bf16[8,2,64,2,256]{4,3,2,1,0:T(2,128)(2,1)S(1)}, bf16[8,2,64,2,256]{4,3,2,1,0:T(2,128)(2,1)S(1)}, u32[]{:S(2)}, u32[]{:S(2)}) %collective-permute-start.2) | collective-permute-done | bytes 1048608 | tf_op jit(solution)/shard_map/ppermute | solution.py:232
  43.3 10.5 %interpolate.5 = (bf16[8,2,64,2,512]{4,3,2,1,0:T(2,128)(2,1)S(1)}, bf16[8,2,64,2,512]{4,3,2,1,0:T(2,128)(2,1)S(1)}, bf16[8,2,64,2,512]{4,3,2,1,0:T(2,128)(2,1)S(1)}, bf16[8,2,64,2,512]{4,3,2,1,0:T(2,128)(2,1)S(1)}) custom-call(bf16[128,256]{1,0:T(8,128)(2,1)S(1)} %fine_weights.1.w_ref, bf16[64,128,2,1280]{3,2,1,0:T(2,128)(2,1)} %g_ref.5), custom_call_target="tpu_custom_call" | custom-call | tf_op jit(solution)/shard_map/interpolate/pallas_call | solution.py:118
  61.7 4.8 %collective-permute-done.7.refs_2_ = bf16[2,64,2,256]{3,2,1,0:T(2,128)(2,1)S(1)} collective-permute-done((bf16[2,64,2,256]{3,2,1,0:T(2,128)(2,1)S(1)}, bf16[2,64,2,256]{3,2,1,0:T(2,128)(2,1)S(1)}, u32[]{:S(2)}, u32[]{:S(2)}) %collective-permute-start.7) | collective-permute-done | bytes 131104 | tf_op jit(solution)/shard_map/ppermute | solution.py:232
  80.0 6.1 %collective-permute-done.9.refs_4_ = bf16[2,64,2,256]{3,2,1,0:T(2,128)(2,1)S(1)} collective-permute-done((bf16[2,64,2,256]{3,2,1,0:T(2,128)(2,1)S(1)}, bf16[2,64,2,256]{3,2,1,0:T(2,128)(2,1)S(1)}, u32[]{:S(2)}, u32[]{:S(2)}) %collective-permute-start.9) | collective-permute-done | bytes 131104 | tf_op jit(solution)/shard_map/ppermute | solution.py:232
  95.2 8.1 %collective-permute-done.11.refs_6_ = bf16[2,64,2,256]{3,2,1,0:T(2,128)(2,1)S(1)} collective-permute-done((bf16[2,64,2,256]{3,2,1,0:T(2,128)(2,1)S(1)}, bf16[2,64,2,256]{3,2,1,0:T(2,128)(2,1)S(1)}, u32[]{:S(2)}, u32[]{:S(2)}) %collective-permute-start.11) | collective-permute-done | bytes 131104 | tf_op jit(solution)/shard_map/ppermute | solution.py:232
  103.2 5.4 %k_phases.1.m_ref = bf16[1024,1024]{1,0:T(8,128)(2,1)S(1)} custom-call(s32[3,512]{1,0:T(4,128)S(1)} %copy-done, s32[3,512]{1,0:T(4,128)S(1)} %copy-done.1), custom_call_target="tpu_custom_call" | custom-call | tf_op jit(solution)/shard_map/k_phases/pallas_call | solution.py:92
  124.9 6.8 %collective-permute-start.17 = (bf16[64,2,2,256]{3,2,1,0:T(2,128)(2,1)S(1)}, bf16[64,2,2,256]{3,2,1,0:T(2,128)(2,1)S(1)}, u32[]{:S(2)}, u32[]{:S(2)}) collective-permute-start(bf16[64,2,2,256]{3,2,1,0:T(2,128)(2,1)S(1)} %get-tuple-element.99), channel_id=1, source_target_pairs={{0,20},{4,16},{8,28},{12,24},{16,4},{20,0},{24,12},{28,8},{1,21},{... | collective-permute-start | bytes 393224 | tf_op jit(solution)/shard_map/ppermute | solution.py:232
  157.9 12.1 %collective-permute-done.40.refs_4_ = bf16[2,64,2,512]{3,2,1,0:T(2,128)(2,1)S(1)} collective-permute-done((bf16[2,64,2,512]{3,2,1,0:T(2,128)(2,1)S(1)}, bf16[2,64,2,512]{3,2,1,0:T(2,128)(2,1)S(1)}, u32[]{:S(2)}, u32[]{:S(2)}) %collective-permute-start.40) | collective-permute-done | bytes 262176 | tf_op jit(solution)/shard_map/ppermute | solution.py:232
  170.0 8.1 %collective-permute-start.21 = (bf16[2,64,2,512]{3,2,1,0:T(2,128)(2,1)S(1)}, bf16[2,64,2,512]{3,2,1,0:T(2,128)(2,1)S(1)}, u32[]{:S(2)}, u32[]{:S(2)}) collective-permute-start(bf16[2,64,2,512]{3,2,1,0:T(2,128)(2,1)S(1)} %get-tuple-element.104), channel_id=1, source_target_pairs={{0,8},{4,12},{8,0},{12,4},{16,24},{20,28},{24,16},{28,20},{1,9},{5... | collective-permute-start | bytes 786440 | tf_op jit(solution)/shard_map/ppermute | solution.py:232
  178.2 6.5 %collective-permute-start.22 = (bf16[2,64,2,512]{3,2,1,0:T(2,128)(2,1)S(1)}, bf16[2,64,2,512]{3,2,1,0:T(2,128)(2,1)S(1)}, u32[]{:S(2)}, u32[]{:S(2)}) collective-permute-start(bf16[2,64,2,512]{3,2,1,0:T(2,128)(2,1)S(1)} %get-tuple-element.105), channel_id=1, source_target_pairs={{0,12},{4,8},{8,4},{12,0},{16,28},{20,24},{24,20},{28,16},{1,13},{... | collective-permute-start | bytes 786440 | tf_op jit(solution)/shard_map/ppermute | solution.py:232
  184.7 5.0 %collective-permute-done.42.refs_6_ = bf16[2,64,2,512]{3,2,1,0:T(2,128)(2,1)S(1)} collective-permute-done((bf16[2,64,2,512]{3,2,1,0:T(2,128)(2,1)S(1)}, bf16[2,64,2,512]{3,2,1,0:T(2,128)(2,1)S(1)}, u32[]{:S(2)}, u32[]{:S(2)}) %collective-permute-start.42) | collective-permute-done | bytes 262176 | tf_op jit(solution)/shard_map/ppermute | solution.py:232
  189.7 9.1 %collective-permute-done.43.refs_7_ = bf16[2,64,2,512]{3,2,1,0:T(2,128)(2,1)S(1)} collective-permute-done((bf16[2,64,2,512]{3,2,1,0:T(2,128)(2,1)S(1)}, bf16[2,64,2,512]{3,2,1,0:T(2,128)(2,1)S(1)}, u32[]{:S(2)}, u32[]{:S(2)}) %collective-permute-start.43) | collective-permute-done | bytes 262176 | tf_op jit(solution)/shard_map/ppermute | solution.py:232
  208.0 10.4 %collective-permute-done.23.refs_4_ = bf16[2,64,2,512]{3,2,1,0:T(2,128)(2,1)S(1)} collective-permute-done((bf16[2,64,2,512]{3,2,1,0:T(2,128)(2,1)S(1)}, bf16[2,64,2,512]{3,2,1,0:T(2,128)(2,1)S(1)}, u32[]{:S(2)}, u32[]{:S(2)}) %collective-permute-start.23) | collective-permute-done | bytes 262176 | tf_op jit(solution)/shard_map/ppermute | solution.py:232
  218.4 4.8 %collective-permute-start.45 = (bf16[64,2,2,512]{3,2,1,0:T(2,128)(2,1)S(1)}, bf16[64,2,2,512]{3,2,1,0:T(2,128)(2,1)S(1)}, u32[]{:S(2)}, u32[]{:S(2)}) collective-permute-start(bf16[64,2,2,512]{3,2,1,0:T(2,128)(2,1)S(1)} %get-tuple-element.132), channel_id=1, source_target_pairs={{0,8},{4,12},{8,0},{12,4},{16,24},{20,28},{24,16},{28,20},{1,9},{5... | collective-permute-start | bytes 786440 | tf_op jit(solution)/shard_map/ppermute | solution.py:232
  224.2 5.6 %collective-permute-start.46 = (bf16[64,2,2,512]{3,2,1,0:T(2,128)(2,1)S(1)}, bf16[64,2,2,512]{3,2,1,0:T(2,128)(2,1)S(1)}, u32[]{:S(2)}, u32[]{:S(2)}) collective-permute-start(bf16[64,2,2,512]{3,2,1,0:T(2,128)(2,1)S(1)} %get-tuple-element.133), channel_id=1, source_target_pairs={{0,12},{4,8},{8,4},{12,0},{16,28},{20,24},{24,20},{28,16},{1,13},{... | collective-permute-start | bytes 786440 | tf_op jit(solution)/shard_map/ppermute | solution.py:232
  235.4 8.4 %collective-permute-done.26.refs_7_ = bf16[2,64,2,512]{3,2,1,0:T(2,128)(2,1)S(1)} collective-permute-done((bf16[2,64,2,512]{3,2,1,0:T(2,128)(2,1)S(1)}, bf16[2,64,2,512]{3,2,1,0:T(2,128)(2,1)S(1)}, u32[]{:S(2)}, u32[]{:S(2)}) %collective-permute-start.26) | collective-permute-done | bytes 262176 | tf_op jit(solution)/shard_map/ppermute | solution.py:232
  253.1 11.4 %collective-permute-done.47.refs_4_ = bf16[64,2,2,512]{3,2,1,0:T(2,128)(2,1)S(1)} collective-permute-done((bf16[64,2,2,512]{3,2,1,0:T(2,128)(2,1)S(1)}, bf16[64,2,2,512]{3,2,1,0:T(2,128)(2,1)S(1)}, u32[]{:S(2)}, u32[]{:S(2)}) %collective-permute-start.47) | collective-permute-done | bytes 262176 | tf_op jit(solution)/shard_map/ppermute | solution.py:232
  270.1 4.6 %collective-permute-start.29 = (bf16[64,2,2,512]{3,2,1,0:T(2,128)(2,1)S(1)}, bf16[64,2,2,512]{3,2,1,0:T(2,128)(2,1)S(1)}, u32[]{:S(2)}, u32[]{:S(2)}) collective-permute-start(bf16[64,2,2,512]{3,2,1,0:T(2,128)(2,1)S(1)} %get-tuple-element.113), channel_id=1, source_target_pairs={{0,12},{4,8},{8,4},{12,0},{16,28},{20,24},{24,20},{28,16},{1,13},{... | collective-permute-start | bytes 786440 | tf_op jit(solution)/shard_map/ppermute | solution.py:232
  277.9 10.8 %collective-permute-done.50.refs_7_ = bf16[64,2,2,512]{3,2,1,0:T(2,128)(2,1)S(1)} collective-permute-done((bf16[64,2,2,512]{3,2,1,0:T(2,128)(2,1)S(1)}, bf16[64,2,2,512]{3,2,1,0:T(2,128)(2,1)S(1)}, u32[]{:S(2)}, u32[]{:S(2)}) %collective-permute-start.50) | collective-permute-done | bytes 262176 | tf_op jit(solution)/shard_map/ppermute | solution.py:232
  293.8 16.6 %collective-permute-done.30.refs_4_ = bf16[64,2,2,512]{3,2,1,0:T(2,128)(2,1)S(1)} collective-permute-done((bf16[64,2,2,512]{3,2,1,0:T(2,128)(2,1)S(1)}, bf16[64,2,2,512]{3,2,1,0:T(2,128)(2,1)S(1)}, u32[]{:S(2)}, u32[]{:S(2)}) %collective-permute-start.30) | collective-permute-done | bytes 262176 | tf_op jit(solution)/shard_map/ppermute | solution.py:232
  310.4 5.6 %collective-permute-done.31.refs_5_ = bf16[64,2,2,512]{3,2,1,0:T(2,128)(2,1)S(1)} collective-permute-done((bf16[64,2,2,512]{3,2,1,0:T(2,128)(2,1)S(1)}, bf16[64,2,2,512]{3,2,1,0:T(2,128)(2,1)S(1)}, u32[]{:S(2)}, u32[]{:S(2)}) %collective-permute-start.31) | collective-permute-done | bytes 262176 | tf_op jit(solution)/shard_map/ppermute | solution.py:232
  316.0 6.3 %collective-permute-done.32.refs_6_ = bf16[64,2,2,512]{3,2,1,0:T(2,128)(2,1)S(1)} collective-permute-done((bf16[64,2,2,512]{3,2,1,0:T(2,128)(2,1)S(1)}, bf16[64,2,2,512]{3,2,1,0:T(2,128)(2,1)S(1)}, u32[]{:S(2)}, u32[]{:S(2)}) %collective-permute-start.32) | collective-permute-done | bytes 262176 | tf_op jit(solution)/shard_map/ppermute | solution.py:232
  (107 shorter events, 129.5 us)
Async XLA Ops:
  53.9 58.2 %collective-permute-start.34 = (bf16[8,2,64,2,512]{4,3,2,1,0:T(2,128)(2,1)S(1)}, bf16[8,2,64,2,512]{4,3,2,1,0:T(2,128)(2,1)S(1)}, u32[]{:S(2)}, u32[]{:S(2)}) collective-permute-start(bf16[8,2,64,2,512]{4,3,2,1,0:T(2,128)(2,1)S(1)} %get-tuple-element.118), channel_id=1, source_target_pairs={{0,1},{1,0},{2,3},{3,2},{4,5},{5,4},{6,7},{7,6},{8,9},{9,8},{10,11... | collective-permute-start | bytes 6291464 | tf_op jit(solution)/shard_map/ppermute | solution.py:232
  56.1 75.6 %collective-permute-start.36 = (bf16[8,2,64,2,512]{4,3,2,1,0:T(2,128)(2,1)S(1)}, bf16[8,2,64,2,512]{4,3,2,1,0:T(2,128)(2,1)S(1)}, u32[]{:S(2)}, u32[]{:S(2)}) collective-permute-start(bf16[8,2,64,2,512]{4,3,2,1,0:T(2,128)(2,1)S(1)} %add_two.5), channel_id=1, source_target_pairs={{0,2},{1,3},{2,0},{3,1},{4,6},{5,7},{6,4},{7,5},{8,10},{9,11},{10,... | collective-permute-start | bytes 6291464 | tf_op jit(solution)/shard_map/ppermute | solution.py:232
  57.6 88.1 %collective-permute-start.3 = (bf16[8,2,64,2,512]{4,3,2,1,0:T(2,128)(2,1)S(1)}, bf16[8,2,64,2,512]{4,3,2,1,0:T(2,128)(2,1)S(1)}, u32[]{:S(2)}, u32[]{:S(2)}) collective-permute-start(bf16[8,2,64,2,512]{4,3,2,1,0:T(2,128)(2,1)S(1)} %get-tuple-element.82), channel_id=1, source_target_pairs={{0,1},{1,0},{2,3},{3,2},{4,5},{5,4},{6,7},{7,6},{8,9},{9,8},{10,11... | collective-permute-start | bytes 6291464 | tf_op jit(solution)/shard_map/ppermute | solution.py:232
  59.7 89.0 %collective-permute-start.5 = (bf16[8,2,64,2,512]{4,3,2,1,0:T(2,128)(2,1)S(1)}, bf16[8,2,64,2,512]{4,3,2,1,0:T(2,128)(2,1)S(1)}, u32[]{:S(2)}, u32[]{:S(2)}) collective-permute-start(bf16[8,2,64,2,512]{4,3,2,1,0:T(2,128)(2,1)S(1)} %add_two.4), channel_id=1, source_target_pairs={{0,2},{1,3},{2,0},{3,1},{4,6},{5,7},{6,4},{7,5},{8,10},{9,11},{10,... | collective-permute-start | bytes 6291464 | tf_op jit(solution)/shard_map/ppermute | solution.py:232
  148.7 29.5 %collective-permute-start.41 = (bf16[2,64,2,512]{3,2,1,0:T(2,128)(2,1)S(1)}, bf16[2,64,2,512]{3,2,1,0:T(2,128)(2,1)S(1)}, u32[]{:S(2)}, u32[]{:S(2)}) collective-permute-start(bf16[2,64,2,512]{3,2,1,0:T(2,128)(2,1)S(1)} %get-tuple-element.127), channel_id=1, source_target_pairs={{0,20},{4,16},{8,28},{12,24},{16,4},{20,0},{24,12},{28,8},{1,21},{... | collective-permute-start | bytes 786440 | tf_op jit(solution)/shard_map/ppermute | solution.py:232
  154.3 35.4 %collective-permute-start.42 = (bf16[2,64,2,512]{3,2,1,0:T(2,128)(2,1)S(1)}, bf16[2,64,2,512]{3,2,1,0:T(2,128)(2,1)S(1)}, u32[]{:S(2)}, u32[]{:S(2)}) collective-permute-start(bf16[2,64,2,512]{3,2,1,0:T(2,128)(2,1)S(1)} %get-tuple-element.128), channel_id=1, source_target_pairs={{0,24},{4,28},{8,16},{12,20},{16,8},{20,12},{24,0},{28,4},{1,25},{... | collective-permute-start | bytes 786440 | tf_op jit(solution)/shard_map/ppermute | solution.py:232
  154.4 44.3 %collective-permute-start.43 = (bf16[2,64,2,512]{3,2,1,0:T(2,128)(2,1)S(1)}, bf16[2,64,2,512]{3,2,1,0:T(2,128)(2,1)S(1)}, u32[]{:S(2)}, u32[]{:S(2)}) collective-permute-start(bf16[2,64,2,512]{3,2,1,0:T(2,128)(2,1)S(1)} %get-tuple-element.129), channel_id=1, source_target_pairs={{0,28},{4,24},{8,20},{12,16},{16,12},{20,8},{24,4},{28,0},{1,29},{... | collective-permute-start | bytes 786440 | tf_op jit(solution)/shard_map/ppermute | solution.py:232
  156.4 42.4 %collective-permute-start.20 = (bf16[2,64,2,512]{3,2,1,0:T(2,128)(2,1)S(1)}, bf16[2,64,2,512]{3,2,1,0:T(2,128)(2,1)S(1)}, u32[]{:S(2)}, u32[]{:S(2)}) collective-permute-start(bf16[2,64,2,512]{3,2,1,0:T(2,128)(2,1)S(1)} %get-tuple-element.103), channel_id=1, source_target_pairs={{0,4},{4,0},{8,12},{12,8},{16,20},{20,16},{24,28},{28,24},{1,5},{5... | collective-permute-start | bytes 786440 | tf_op jit(solution)/shard_map/ppermute | solution.py:232
  170.0 31.5 %collective-permute-start.21 = (bf16[2,64,2,512]{3,2,1,0:T(2,128)(2,1)S(1)}, bf16[2,64,2,512]{3,2,1,0:T(2,128)(2,1)S(1)}, u32[]{:S(2)}, u32[]{:S(2)}) collective-permute-start(bf16[2,64,2,512]{3,2,1,0:T(2,128)(2,1)S(1)} %get-tuple-element.104), channel_id=1, source_target_pairs={{0,8},{4,12},{8,0},{12,4},{16,24},{20,28},{24,16},{28,20},{1,9},{5... | collective-permute-start | bytes 786440 | tf_op jit(solution)/shard_map/ppermute | solution.py:232
  178.2 29.7 %collective-permute-start.22 = (bf16[2,64,2,512]{3,2,1,0:T(2,128)(2,1)S(1)}, bf16[2,64,2,512]{3,2,1,0:T(2,128)(2,1)S(1)}, u32[]{:S(2)}, u32[]{:S(2)}) collective-permute-start(bf16[2,64,2,512]{3,2,1,0:T(2,128)(2,1)S(1)} %get-tuple-element.105), channel_id=1, source_target_pairs={{0,12},{4,8},{8,4},{12,0},{16,28},{20,24},{24,20},{28,16},{1,13},{... | collective-permute-start | bytes 786440 | tf_op jit(solution)/shard_map/ppermute | solution.py:232
  189.7 28.7 %collective-permute-start.23 = (bf16[2,64,2,512]{3,2,1,0:T(2,128)(2,1)S(1)}, bf16[2,64,2,512]{3,2,1,0:T(2,128)(2,1)S(1)}, u32[]{:S(2)}, u32[]{:S(2)}) collective-permute-start(bf16[2,64,2,512]{3,2,1,0:T(2,128)(2,1)S(1)} %get-tuple-element.106), channel_id=1, source_target_pairs={{0,16},{4,20},{8,24},{12,28},{16,0},{20,4},{24,8},{28,12},{1,17},{... | collective-permute-start | bytes 786440 | tf_op jit(solution)/shard_map/ppermute | solution.py:232
  198.8 35.0 %collective-permute-start.25 = (bf16[2,64,2,512]{3,2,1,0:T(2,128)(2,1)S(1)}, bf16[2,64,2,512]{3,2,1,0:T(2,128)(2,1)S(1)}, u32[]{:S(2)}, u32[]{:S(2)}) collective-permute-start(bf16[2,64,2,512]{3,2,1,0:T(2,128)(2,1)S(1)} %get-tuple-element.108), channel_id=1, source_target_pairs={{0,24},{4,28},{8,16},{12,20},{16,8},{20,12},{24,0},{28,4},{1,25},{... | collective-permute-start | bytes 786440 | tf_op jit(solution)/shard_map/ppermute | solution.py:232
  201.6 42.2 %collective-permute-start.26 = (bf16[2,64,2,512]{3,2,1,0:T(2,128)(2,1)S(1)}, bf16[2,64,2,512]{3,2,1,0:T(2,128)(2,1)S(1)}, u32[]{:S(2)}, u32[]{:S(2)}) collective-permute-start(bf16[2,64,2,512]{3,2,1,0:T(2,128)(2,1)S(1)} %get-tuple-element.109), channel_id=1, source_target_pairs={{0,28},{4,24},{8,20},{12,16},{16,12},{20,8},{24,4},{28,0},{1,29},{... | collective-permute-start | bytes 786440 | tf_op jit(solution)/shard_map/ppermute | solution.py:232
  208.0 38.9 %collective-permute-start.44 = (bf16[64,2,2,512]{3,2,1,0:T(2,128)(2,1)S(1)}, bf16[64,2,2,512]{3,2,1,0:T(2,128)(2,1)S(1)}, u32[]{:S(2)}, u32[]{:S(2)}) collective-permute-start(bf16[64,2,2,512]{3,2,1,0:T(2,128)(2,1)S(1)} %get-tuple-element.131), channel_id=1, source_target_pairs={{0,4},{4,0},{8,12},{12,8},{16,20},{20,16},{24,28},{28,24},{1,5},{5... | collective-permute-start | bytes 786440 | tf_op jit(solution)/shard_map/ppermute | solution.py:232
  218.4 31.1 %collective-permute-start.45 = (bf16[64,2,2,512]{3,2,1,0:T(2,128)(2,1)S(1)}, bf16[64,2,2,512]{3,2,1,0:T(2,128)(2,1)S(1)}, u32[]{:S(2)}, u32[]{:S(2)}) collective-permute-start(bf16[64,2,2,512]{3,2,1,0:T(2,128)(2,1)S(1)} %get-tuple-element.132), channel_id=1, source_target_pairs={{0,8},{4,12},{8,0},{12,4},{16,24},{20,28},{24,16},{28,20},{1,9},{5... | collective-permute-start | bytes 786440 | tf_op jit(solution)/shard_map/ppermute | solution.py:232
  224.2 28.9 %collective-permute-start.46 = (bf16[64,2,2,512]{3,2,1,0:T(2,128)(2,1)S(1)}, bf16[64,2,2,512]{3,2,1,0:T(2,128)(2,1)S(1)}, u32[]{:S(2)}, u32[]{:S(2)}) collective-permute-start(bf16[64,2,2,512]{3,2,1,0:T(2,128)(2,1)S(1)} %get-tuple-element.133), channel_id=1, source_target_pairs={{0,12},{4,8},{8,4},{12,0},{16,28},{20,24},{24,20},{28,16},{1,13},{... | collective-permute-start | bytes 786440 | tf_op jit(solution)/shard_map/ppermute | solution.py:232
  233.8 30.7 %collective-permute-start.47 = (bf16[64,2,2,512]{3,2,1,0:T(2,128)(2,1)S(1)}, bf16[64,2,2,512]{3,2,1,0:T(2,128)(2,1)S(1)}, u32[]{:S(2)}, u32[]{:S(2)}) collective-permute-start(bf16[64,2,2,512]{3,2,1,0:T(2,128)(2,1)S(1)} %get-tuple-element.134), channel_id=1, source_target_pairs={{0,16},{4,20},{8,24},{12,28},{16,0},{20,4},{24,8},{28,12},{1,17},{... | collective-permute-start | bytes 786440 | tf_op jit(solution)/shard_map/ppermute | solution.py:232
  246.8 31.1 %collective-permute-start.49 = (bf16[64,2,2,512]{3,2,1,0:T(2,128)(2,1)S(1)}, bf16[64,2,2,512]{3,2,1,0:T(2,128)(2,1)S(1)}, u32[]{:S(2)}, u32[]{:S(2)}) collective-permute-start(bf16[64,2,2,512]{3,2,1,0:T(2,128)(2,1)S(1)} %get-tuple-element.136), channel_id=1, source_target_pairs={{0,24},{4,28},{8,16},{12,20},{16,8},{20,12},{24,0},{28,4},{1,25},{... | collective-permute-start | bytes 786440 | tf_op jit(solution)/shard_map/ppermute | solution.py:232
  249.5 39.2 %collective-permute-start.50 = (bf16[64,2,2,512]{3,2,1,0:T(2,128)(2,1)S(1)}, bf16[64,2,2,512]{3,2,1,0:T(2,128)(2,1)S(1)}, u32[]{:S(2)}, u32[]{:S(2)}) collective-permute-start(bf16[64,2,2,512]{3,2,1,0:T(2,128)(2,1)S(1)} %get-tuple-element.137), channel_id=1, source_target_pairs={{0,28},{4,24},{8,20},{12,16},{16,12},{20,8},{24,4},{28,0},{1,29},{... | collective-permute-start | bytes 786440 | tf_op jit(solution)/shard_map/ppermute | solution.py:232
  253.0 35.6 %collective-permute-start.27 = (bf16[64,2,2,512]{3,2,1,0:T(2,128)(2,1)S(1)}, bf16[64,2,2,512]{3,2,1,0:T(2,128)(2,1)S(1)}, u32[]{:S(2)}, u32[]{:S(2)}) collective-permute-start(bf16[64,2,2,512]{3,2,1,0:T(2,128)(2,1)S(1)} %get-tuple-element.111), channel_id=1, source_target_pairs={{0,4},{4,0},{8,12},{12,8},{16,20},{20,16},{24,28},{28,24},{1,5},{5... | collective-permute-start | bytes 786440 | tf_op jit(solution)/shard_map/ppermute | solution.py:232
  277.9 32.5 %collective-permute-start.30 = (bf16[64,2,2,512]{3,2,1,0:T(2,128)(2,1)S(1)}, bf16[64,2,2,512]{3,2,1,0:T(2,128)(2,1)S(1)}, u32[]{:S(2)}, u32[]{:S(2)}) collective-permute-start(bf16[64,2,2,512]{3,2,1,0:T(2,128)(2,1)S(1)} %get-tuple-element.114), channel_id=1, source_target_pairs={{0,16},{4,20},{8,24},{12,28},{16,0},{20,4},{24,8},{28,12},{1,17},{... | collective-permute-start | bytes 786440 | tf_op jit(solution)/shard_map/ppermute | solution.py:232
  288.7 27.3 %collective-permute-start.31 = (bf16[64,2,2,512]{3,2,1,0:T(2,128)(2,1)S(1)}, bf16[64,2,2,512]{3,2,1,0:T(2,128)(2,1)S(1)}, u32[]{:S(2)}, u32[]{:S(2)}) collective-permute-start(bf16[64,2,2,512]{3,2,1,0:T(2,128)(2,1)S(1)} %get-tuple-element.115), channel_id=1, source_target_pairs={{0,20},{4,16},{8,28},{12,24},{16,4},{20,0},{24,12},{28,8},{1,21},{... | collective-permute-start | bytes 786440 | tf_op jit(solution)/shard_map/ppermute | solution.py:232
  288.7 33.6 %collective-permute-start.32 = (bf16[64,2,2,512]{3,2,1,0:T(2,128)(2,1)S(1)}, bf16[64,2,2,512]{3,2,1,0:T(2,128)(2,1)S(1)}, u32[]{:S(2)}, u32[]{:S(2)}) collective-permute-start(bf16[64,2,2,512]{3,2,1,0:T(2,128)(2,1)S(1)} %get-tuple-element.116), channel_id=1, source_target_pairs={{0,24},{4,28},{8,16},{12,20},{16,8},{20,12},{24,0},{28,4},{1,25},{... | collective-permute-start | bytes 786440 | tf_op jit(solution)/shard_map/ppermute | solution.py:232
  290.0 36.6 %collective-permute-start.33 = (bf16[64,2,2,512]{3,2,1,0:T(2,128)(2,1)S(1)}, bf16[64,2,2,512]{3,2,1,0:T(2,128)(2,1)S(1)}, u32[]{:S(2)}, u32[]{:S(2)}) collective-permute-start(bf16[64,2,2,512]{3,2,1,0:T(2,128)(2,1)S(1)} %get-tuple-element.117), channel_id=1, source_target_pairs={{0,28},{4,24},{8,20},{12,16},{16,12},{20,8},{24,4},{28,0},{1,29},{... | collective-permute-start | bytes 786440 | tf_op jit(solution)/shard_map/ppermute | solution.py:232
  (33 other events, 450.5 us)
